TPU v7x, 128 devices: a whole 4x4x4 slice. The times are simulated.
128 devices in a mesh: rep: 16 (over y, z), grp: 8 (over x, core).
Axes of the slice: x: 4, y: 4, z: 4, core: 2. Of those that a mesh axis runs over, the one named last changes fastest.
Arguments:
- grad_query: float32 [16, 2048, 2048], P('rep', 'grp'), may hold values from -100 to 100, as said below
- error_query: float32 [16, 2048, 2048], P('rep', 'grp'), may hold values from -3 to 3
- basis_query: float32 [2048, 32], replicated, may hold values from -0.125 to 0.125
- momentum_query: float32 [2048, 2048], P('grp'), may hold values from -0.6 to 0.6
- master_query: float32 [2048, 2048], P('grp'), may hold values from -6 to 6
- grad_gate: float32 [16, 2048, 256], P('rep', 'grp'), may hold values from -100 to 100, as said below
- error_gate: float32 [16, 2048, 256], P('rep', 'grp'), may hold values from -3 to 3
- basis_gate: float32 [256, 32], replicated, may hold values from -0.375 to 0.375
- momentum_gate: float32 [2048, 256], P('grp'), may hold values from -0.6 to 0.6
- master_gate: float32 [2048, 256], P('grp'), may hold values from -6 to 6
- vector_grad: float32 [16, 12800], P('rep', 'grp'), may hold values from -6 to 6
- vector_momentum: float32 [12800], P('grp'), may hold values from -0.6 to 0.6
- vector_master: float32 [12800], P('grp'), may hold values from 0.5 to 1.5
Outputs:
- new_error_query: float32 [16, 2048, 2048], P('rep', 'grp')
- new_momentum_query: float32 [2048, 2048], P('grp')
- new_master_query: float32 [2048, 2048], P('grp')
- weight_query: bfloat16 [2048, 2048], replicated
- new_basis_query: float32 [2048, 32], replicated
- new_error_gate: float32 [16, 2048, 256], P('rep', 'grp')
- new_momentum_gate: float32 [2048, 256], P('grp')
- new_master_gate: float32 [2048, 256], P('grp')
- weight_gate: bfloat16 [2048, 256], replicated
- new_basis_gate: float32 [256, 32], replicated
- new_vector_momentum: float32 [12800], P('grp')
- new_vector_master: float32 [12800], P('grp')
- weight_vector: bfloat16 [12800], replicated
Inputs may be any that keep to these rules, and one draw needn't show every extreme that they name: `grad_query`: each replica's gradient is a common part plus a replica's own part. `grad_gate`: each replica's gradient is a common part plus a replica's own part.
All inputs are finite; a program needn't handle non-finite values.
Results may differ from a plain program's by a relative error of at most 0.0006.
Values may be sent and summed in bfloat16 or wider, within the bound.
A program may use at most 128 MiB of HBM per device.

v0:
```python
import jax
import jax.numpy as jnp
from jax import lax
from jax.sharding import PartitionSpec as P

NS_STEPS = 4


highest = lax.Precision.HIGHEST


def inverse_root(gram_matrix):
    trace_value = jnp.trace(gram_matrix)
    identity = jnp.eye(gram_matrix.shape[0], dtype=jnp.float32)
    root_part = gram_matrix / trace_value
    inverse_part = identity
    for iteration in range(NS_STEPS):
        middle = 0.5 * (3.0 * identity - jnp.dot(inverse_part, root_part, precision=highest))
        root_part = jnp.dot(root_part, middle, precision=highest)
        inverse_part = jnp.dot(middle, inverse_part, precision=highest)
    return inverse_part / jnp.sqrt(trace_value)


def right_terms(merged, ortho):
    return jnp.einsum("dn,dr->nr", merged, ortho, precision=highest)


def finish(merged, ortho, new_basis, momentum, master, replicas):
    approx = jnp.dot(ortho, new_basis.T, precision=highest) / replicas
    new_error = (merged - approx)[None]
    new_momentum = 0.9 * momentum + approx
    new_master = master - 0.5 * new_momentum
    return (new_error, new_momentum, new_master)


def per_device(
    grad_query,
    error_query,
    basis_query,
    momentum_query,
    master_query,
    grad_gate,
    error_gate,
    basis_gate,
    momentum_gate,
    master_gate,
    vector_grad,
    vector_momentum,
    vector_master,
):
    replicas = lax.axis_size("rep")
    merged_query = (grad_query + error_query)[0]
    merged_gate = (grad_gate + error_gate)[0]
    local_query = jnp.dot(merged_query, basis_query, precision=highest)
    local_gate = jnp.dot(merged_gate, basis_gate, precision=highest)
    vector_local = vector_grad[0]
    vector_total = lax.psum(vector_local, "rep")
    left_query, left_gate = lax.psum((local_query, local_gate), "rep")
    gram_query, gram_gate = lax.psum(
        (
            jnp.dot(left_query.T, left_query, precision=highest),
            jnp.dot(left_gate.T, left_gate, precision=highest),
        ),
        "grp",
    )
    ortho_query = jnp.dot(left_query, inverse_root(gram_query), precision=highest)
    ortho_gate = jnp.dot(left_gate, inverse_root(gram_gate), precision=highest)
    terms_query = right_terms(merged_query, ortho_query)
    terms_gate = right_terms(merged_gate, ortho_gate)
    basis_new_query, basis_new_gate = lax.psum((terms_query, terms_gate), ("rep", "grp"))
    error_out_query, momentum_out_query, master_out_query = finish(
        merged_query, ortho_query, basis_new_query, momentum_query, master_query, replicas
    )
    error_out_gate, momentum_out_gate, master_out_gate = finish(
        merged_gate, ortho_gate, basis_new_gate, momentum_gate, master_gate, replicas
    )
    vector_mean = vector_total / replicas
    momentum_out_vector = 0.9 * vector_momentum + vector_mean
    master_out_vector = vector_master - 0.5 * momentum_out_vector
    whole_query, whole_gate, whole_vector = (
        lax.all_gather(master_out_query.astype(jnp.bfloat16), "grp", axis=0, tiled=True),
        lax.all_gather(master_out_gate.astype(jnp.bfloat16), "grp", axis=0, tiled=True),
        lax.all_gather(master_out_vector.astype(jnp.bfloat16), "grp", axis=0, tiled=True),
    )
    return (
        error_out_query,
        momentum_out_query,
        master_out_query,
        whole_query,
        basis_new_query,
        error_out_gate,
        momentum_out_gate,
        master_out_gate,
        whole_gate,
        basis_new_gate,
        momentum_out_vector,
        master_out_vector,
        whole_vector,
    )


def solution(mesh):
    in_specs = (
        P("rep", "grp", None),
        P("rep", "grp", None),
        P(),
        P("grp", None),
        P("grp", None),
        P("rep", "grp", None),
        P("rep", "grp", None),
        P(),
        P("grp", None),
        P("grp", None),
        P("rep", "grp"),
        P("grp"),
        P("grp"),
    )
    out_specs = (
        P("rep", "grp", None),
        P("grp", None),
        P("grp", None),
        P(),
        P(),
        P("rep", "grp", None),
        P("grp", None),
        P("grp", None),
        P(),
        P(),
        P("grp"),
        P("grp"),
        P(),
    )
    return jax.shard_map(
        per_device, mesh=mesh, in_specs=in_specs, out_specs=out_specs, check_vma=False
    )
```

profile of v0, /device:TPU:1, one launch (start us, length us, event | category | flops | bytes accessed | tf_op | source)
XLA Modules:
  0.0 369.3 jit_solution(9648238144526546208)
XLA Ops:
  7.2 0.0 copy-start
  7.2 0.0 all-reduce.8.cloned.1.call-start
  7.2 1.3 reduce
  8.6 0.0 copy-start.1
  8.6 4.9 %fusion.2 = f32[256,32]{0,1:T(8,128)} fusion(f32[2048,32]{0,1:T(8,128)S(1)} %copy-done, f32[1,256,2048]{2,1,0:T(8,128)} %param.13, f32[1,256,2048]{2,1,0:T(8,128)} %param.14), kind=kOutput, calls=%fused_computation.4 | convolution fusion | flops 201850880 | bytes 4489216 | tf_op jit(solution)/shard_map/dot_general | solution.py:54
  13.5 0.0 copy-done.3
  13.5 1.0 fusion.15
  14.4 0.0 all-reduce.8.cloned.1.call-update
  14.5 0.0 all-reduce.6.cloned.1.call-start
  14.5 83.3 %all-reduce.8.cloned.1.call-done = (f32[256,32]{0,1:T(8,128)}, f32[256,32]{0,1:T(8,128)}, f32[1600]{0:T(1024)}) async-done(((f32[256,32]{0,1:T(8,128)}, f32[256,32]{0,1:T(8,128)}, f32[1600]{0:T(1024)}), (f32[256,32]{0,1:T(8,128)}, f32[256,32]{0,1:T(8,128)}, f32[1600]{0:T(1024)})) %all-reduce.8.cloned.1.call-update) | async-done | bytes 71952 | tf_op jit(solution)/shard_map/psum | solution.py:58
  97.8 1.0 fusion.29
  98.8 1.0 fusion.35
  99.8 22.7 %all-reduce.2 = (f32[32,32]{1,0:T(8,128)S(1)}, f32[32,32]{1,0:T(8,128)S(1)}) all-reduce(f32[32,32]{1,0:T(8,128)S(1)} %fusion.29, f32[32,32]{1,0:T(8,128)S(1)} %fusion.35), channel_id=1, replica_groups=mesh['rep'=16,'grp'=8] {'grp'}, use_global_device_ids=true, to_apply=%region_1.0 | all-reduce | flops 2048 | bytes 16384 | tf_op jit(solution)/shard_map/psum | solution.py:59
  122.5 0.6 select_reduce_fusion
  123.1 0.8 fusion.12
  123.9 0.1 fusion.19
  124.0 0.8 fusion.20
  124.8 0.2 fusion.11
  125.0 0.1 fusion.30
  125.1 0.1 fusion.31
  125.3 0.2 fusion.10
  125.4 0.1 fusion.32
  125.6 0.1 fusion.33
  126.5 0.8 fusion.8
  127.2 0.1 fusion.18
  127.4 0.8 fusion.21
  128.2 0.2 fusion.7
  128.3 0.1 fusion.36
  128.5 0.1 fusion.37
  128.6 0.2 fusion.6
  128.8 0.1 fusion.38
  128.9 0.1 fusion.39
  129.8 0.1 fusion.9
  129.9 0.1 convolution_divide_fusion.1
  130.1 1.0 fusion.34
  131.1 0.0 copy-done.1
  131.1 0.0 copy-start.6
  131.1 0.0 copy-start.7
  131.1 0.0 copy-start.8
  131.1 3.8 %fusion = f32[2048,32]{0,1:T(8,128)} fusion(f32[256,32]{0,1:T(8,128)S(1)} %fusion.34, f32[1,256,2048]{2,1,0:T(8,128)S(1)} %copy-done.1, f32[1,256,2048]{2,1,0:T(8,128)} %param.14), kind=kOutput, calls=%fused_computation.2 | convolution fusion | flops 201850880 | bytes 4489216 | tf_op jit(solution)/shard_map/dn,dr->nr/dot_general | solution.py:25
  134.9 0.0 all-reduce.6.cloned.1.call-update
  134.9 0.0 all-gather.5.cloned.1.call-start
  134.9 0.1 fusion.5
  135.1 0.1 convolution_divide_fusion
  135.3 0.2 fusion.40
  135.5 0.3 fusion.13
  135.8 65.4 %psum.54 = f32[256,32]{0,1:T(8,128)S(1)} all-reduce(f32[256,32]{0,1:T(8,128)S(1)} %fusion.13), channel_id=1, replica_groups=mesh['rep'=16,'grp'=8] {'rep','grp'}, use_global_device_ids=true, to_apply=%region_7.8 | all-reduce | flops 8192 | bytes 65536 | tf_op jit(solution)/shard_map/psum | solution.py:70
  201.2 1.5 fusion.27
  202.6 0.0 all-gather.5.cloned.1.call-update
  202.7 0.0 copy-start.14
  202.7 0.0 copy-start.11
  202.7 0.0 copy-start.12
  202.7 0.0 all-gather.3.cloned.1.call-start
  202.8 74.1 %all-reduce.6.cloned.1.call-done = f32[2048,32]{0,1:T(8,128)} async-done(((f32[2048,32]{0,1:T(8,128)}), f32[2048,32]{0,1:T(8,128)}) %all-reduce.6.cloned.1.call-update) | async-done | bytes 262160 | tf_op jit(solution)/shard_map/psum | solution.py:70
  276.8 8.2 %fusion.28 = (bf16[256,2048]{1,0:T(8,128)(2,1)}, f32[256,2048]{1,0:T(8,128)}, f32[256,2048]{1,0:T(8,128)}, f32[1,256,2048]{2,1,0:T(8,128)}) fusion(f32[256,2048]{1,0:T(8,128)} %param.17, f32[256,2048]{1,0:T(8,128)} %param.16, f32[1,256,2048]{2,1,0:T(8,128)S(1)} %copy-done.1, f32[1,256,2048]{2,1,0:T(8,128)} %param.14, f32[256,32]{0,1:T(8,128)S(1)} %fusion.34, ...), kind=kOutput, calls=%fused_computation.53 | convolution fusion | flops 205520896 | bytes 16023552 | tf_op jit(solution)/shard_map/dot_general | solution.py:29
  285.1 0.0 all-gather.3.cloned.1.call-update
  285.1 0.6 dynamic-slice
  286.4 0.6 fusion.26
  287.0 0.2 dynamic-update-slice
  287.3 22.5 %all-reduce = bf16[12800]{0:T(1024)(128)(2,1)} all-reduce(bf16[12800]{0:T(1024)(128)(2,1)S(1)} %dynamic-update-slice), channel_id=1, replica_groups=mesh['rep'=16,'grp'=8] {'grp'}, use_global_device_ids=true, to_apply=%add | all-reduce | flops 12800 | bytes 51200
  309.7 42.8 %all-gather.3.cloned.1.call-done = bf16[2048,2048]{1,0:T(8,128)(2,1)} async-done(((bf16[256,2048]{1,0:T(8,128)(2,1)}), bf16[2048,2048]{1,0:T(8,128)(2,1)}) %all-gather.3.cloned.1.call-update) | async-done | bytes 8388624 | tf_op jit(solution)/shard_map/all_gather | solution.py:81
  352.5 8.5 %copy.33 = bf16[2048,2048]{1,0:T(8,128)(2,1)} copy(bf16[2048,2048]{1,0:T(8,128)(2,1)} %all-gather.3.cloned.1.call-done) | data formatting | bytes 16777216
  361.1 0.7 copy.34
  361.8 1.0 copy.35
  (22 shorter events, 0.0 us)
Async XLA Ops:
  7.2 1.4 copy-start
  7.2 90.6 %all-reduce.8.cloned.1.call-start = ((), (), s32[]{:S(2)}) async-start(), calls=%async_computation.3 | async-start | bytes 147456 | tf_op jit(solution)/shard_map/psum | solution.py:58
  8.6 4.9 %copy-start.2 = (f32[1,256,256]{2,1,0:T(8,128)S(1)}, f32[1,256,256]{2,1,0:T(8,128)}, u32[]{:S(2)}) copy-start(f32[1,256,256]{2,1,0:T(8,128)} %param.18) | copy-start | bytes 786436
  8.6 4.9 %copy-start.3 = (f32[1,256,256]{2,1,0:T(8,128)S(1)}, f32[1,256,256]{2,1,0:T(8,128)}, u32[]{:S(2)}) copy-start(f32[1,256,256]{2,1,0:T(8,128)} %param.19) | copy-start | bytes 786436
  8.6 4.9 %copy-start.10 = (f32[256,32]{0,1:T(8,128)S(1)}, f32[256,32]{0,1:T(8,128)}, u32[]{:S(2)}) copy-start(f32[256,32]{0,1:T(8,128)} %param.20) | copy-start | bytes 98308
  8.6 122.5 %copy-start.1 = (f32[1,256,2048]{2,1,0:T(8,128)S(1)}, f32[1,256,2048]{2,1,0:T(8,128)}, u32[]{:S(2)}) copy-start(f32[1,256,2048]{2,1,0:T(8,128)} %param.13) | copy-start | bytes 6291460
  14.5 262.4 %all-reduce.6.cloned.1.call-start = ((), (), s32[]{:S(2)}) async-start(), calls=%async_computation | async-start | bytes 524288 | tf_op jit(solution)/shard_map/psum | solution.py:70
  131.1 4.2 %copy-start.6 = (f32[256,32]{0,1:T(8,128)S(1)}, f32[256,32]{0,1:T(8,128)}, u32[]{:S(2)}) copy-start(f32[256,32]{0,1:T(8,128)} %get-tuple-element.14) | copy-start | bytes 98308
  131.1 70.1 %copy-start.7 = (f32[256,256]{1,0:T(8,128)S(1)}, f32[256,256]{1,0:T(8,128)}, u32[]{:S(2)}) copy-start(f32[256,256]{1,0:T(8,128)} %param.22) | copy-start | bytes 786436
  131.1 70.1 %copy-start.8 = (f32[256,256]{1,0:T(8,128)S(1)}, f32[256,256]{1,0:T(8,128)}, u32[]{:S(2)}) copy-start(f32[256,256]{1,0:T(8,128)} %param.21) | copy-start | bytes 786436
  134.9 174.8 %all-gather.5.cloned.1.call-start = ((), (), s32[]{:S(2)}) async-start(), calls=%async_computation.2 | async-start | bytes 1179648 | tf_op jit(solution)/shard_map/all_gather | solution.py:82
  201.2 83.9 %copy-start.9 = (f32[256,32]{0,1:T(8,128)}, f32[256,32]{0,1:T(8,128)S(1)}, u32[]{:S(2)}) copy-start(f32[256,32]{0,1:T(8,128)S(1)} %psum.54) | copy-start | bytes 98308
  202.7 82.5 %copy-start.14 = (u32[128]{0:T(128)S(1)}, u32[128]{0:T(128)}, u32[]{:S(2)}) copy-start(u32[128]{0:T(128)} %constant.33) | copy-start | bytes 1540
  202.7 83.7 %copy-start.11 = (f32[1600]{0:T(1024)S(1)}, f32[1600]{0:T(1024)}, u32[]{:S(2)}) copy-start(f32[1600]{0:T(1024)} %param.25) | copy-start | bytes 19204
  202.7 83.7 %copy-start.12 = (f32[1600]{0:T(1024)S(1)}, f32[1600]{0:T(1024)}, u32[]{:S(2)}) copy-start(f32[1600]{0:T(1024)} %param.24) | copy-start | bytes 19204
  202.7 83.7 %copy-start.13 = (f32[1600]{0:T(1024)S(1)}, f32[1600]{0:T(1024)}, u32[]{:S(2)}) copy-start(f32[1600]{0:T(1024)} %get-tuple-element.15) | copy-start | bytes 19204
  202.7 149.8 %all-gather.3.cloned.1.call-start = ((), (), s32[]{:S(2)}) async-start(), calls=%async_computation.1 | async-start | bytes 9437184 | tf_op jit(solution)/shard_map/all_gather | solution.py:81
  352.5 8.6 %copy-start.4 = (f32[2048,32]{0,1:T(8,128)S(1)}, f32[2048,32]{0,1:T(8,128)}, u32[]{:S(2)}) copy-start(f32[2048,32]{0,1:T(8,128)} %all-reduce.6.cloned.1.call-done) | copy-start | bytes 786436
  352.5 9.3 %copy-start.5 = (bf16[2048,256]{1,0:T(8,128)(2,1)S(1)}, bf16[2048,256]{1,0:T(8,128)(2,1)}, u32[]{:S(2)}) copy-start(bf16[2048,256]{1,0:T(8,128)(2,1)} %all-gather.5.cloned.1.call-done) | copy-start | bytes 3145732
Sparse Core Ops, SparseCore 0:
  14.6 83.1 all-reduce.7
  135.0 141.7 all-reduce.5
  279.3 21.1 all-gather.4
  302.7 49.7 all-gather.2
where the time goes:
time: 370 us; the launch traced here: 369 us
  waiting for transfers between devices  200 us (54%)
  blocking collectives  111 us (30%)
  matrix products  28.5 us (8%)
  between operations  16.1 us (4%)
  local copies, waits for them, and re-layouts  11.1 us (3%)
    psum x1, waiting for transfers between devices, per_device(): left_query, left_gate = lax.psum((local_query, local_gate), 'rep')  83.3 us
    psum x1, waiting for transfers between devices, per_device(): lax.psum((terms_query, terms_gate), ('rep', 'grp'))  74.1 us
    psum x1, blocking collectives, per_device(): lax.psum((terms_query, terms_gate), ('rep', 'grp'))  65.4 us
    all_gather x1, waiting for transfers between devices, per_device(): lax.all_gather(master_out_query.astype(jnp.bfloat16), 'grp', axis=0, tile...  42.8 us
    psum x1, blocking collectives, per_device(): lax.psum((jnp.dot(left_query.T, left_query, precision=highest), jnp.dot(l...  22.7 us
    unnamed x1, blocking collectives  22.5 us
    unnamed x36, local copies, waits for them, and re-layouts  11.1 us
    dot_general x2, matrix products, finish(): approx = jnp.dot(ortho, new_basis.T, precision=highest) / replicas  9.7 us
  transfers between devices with their start and end apart: 4, of which 3 were waited for; matrix products, arithmetic and copies ran while one was open for 3% of the time, Pallas kernels for 0%

commit v1 on v0

v1 whole, which is shorter than its diff:
```python
import functools

import jax
import jax.numpy as jnp
from jax import lax
from jax.experimental import pallas as pl
from jax.experimental.pallas import tpu as pltpu
from jax.sharding import PartitionSpec as P

NS_STEPS = 4
RANK = 32
BOTH = 2 * RANK
HIGHEST = lax.Precision.HIGHEST
F32 = jnp.float32
BF16 = jnp.bfloat16
VMEM = pltpu.VMEM
NT = (((1,), (1,)), ((), ()))


def split(x):
    high = x.astype(BF16)
    return high, (x - high.astype(F32)).astype(BF16)


def mm(a, b, dims=(((1,), (0,)), ((), ()))):
    return lax.dot_general(a, b, dims, preferred_element_type=F32)


def three_pass(a_high, a_low, b_high, b_low, dims=(((1,), (0,)), ((), ()))):
    rows = a_high.shape[0]
    both = mm(jnp.concatenate([a_high, a_low], axis=0), b_high, dims)
    return both[:rows] + both[rows:] + mm(a_high, b_low, dims)


def full_dot(a, b):
    return jnp.dot(a, b, precision=HIGHEST, preferred_element_type=F32)


def inverse_roots(query_gram, gate_gram):
    row = lax.broadcasted_iota(jnp.int32, (BOTH, BOTH), 0)
    column = lax.broadcasted_iota(jnp.int32, (BOTH, BOTH), 1)
    identity = (row == column).astype(F32)
    zero = jnp.zeros((RANK, RANK), F32)
    gram = jnp.concatenate(
        [
            jnp.concatenate([query_gram, zero], axis=1),
            jnp.concatenate([zero, gate_gram], axis=1),
        ],
        axis=0,
    )
    diagonal = jnp.sum(gram * identity, axis=1, keepdims=True)
    is_query = lax.broadcasted_iota(jnp.int32, (BOTH, 1), 0) < RANK
    query_trace = jnp.sum(jnp.where(is_query, diagonal, 0.0), axis=0, keepdims=True)
    gate_trace = jnp.sum(jnp.where(is_query, 0.0, diagonal), axis=0, keepdims=True)
    trace = jnp.where(is_query, query_trace, gate_trace)
    root = gram / trace
    middle = 0.5 * (3.0 * identity - root)
    inverse = middle
    for step in range(1, NS_STEPS):
        root = full_dot(root, middle)
        middle = 0.5 * (3.0 * identity - full_dot(inverse, root))
        inverse = full_dot(middle, inverse)
    return inverse / jnp.sqrt(trace)


def factor_kernel(
    reps,
    grps,
    grad_query,
    error_query,
    basis_query,
    grad_gate,
    error_gate,
    basis_gate,
    vector_grad,
    vector_momentum,
    vector_master,
    ortho_out,
    right_out,
    momentum_out,
    master_out,
    weight_out,
    grad_in,
    error_in,
    merged_high,
    merged_low,
    left_send,
    left_recv,
    left_sum,
    left_all,
    left,
    gram_all,
    vector_rows,
    vector_send,
    vector_all,
    vector_place,
    right_send,
    right_recv,
    right_part,
    right_final,
    right_all,
    load_sem,
    rep_send,
    rep_recv,
    grp_send,
    grp_recv,
):
    me = lax.axis_index("rep")
    my = lax.axis_index("grp")
    columns = grad_query.shape[1]
    gate = grad_gate.shape[1]
    step = 512
    pieces = [(i * step, step, i) for i in range(columns // step)]
    pieces.append((columns, gate, len(pieces)))

    def loads(start, size, index):
        if start < columns:
            grad, error, place = grad_query, error_query, pl.ds(start, size)
        else:
            grad, error, place = grad_gate, error_gate, pl.ds(0, size)
        into = pl.ds(start, size)
        return (
            pltpu.make_async_copy(
                grad.at[:, place], grad_in.at[:, into], load_sem.at[0, index]
            ),
            pltpu.make_async_copy(
                error.at[:, place], error_in.at[:, into], load_sem.at[1, index]
            ),
        )

    for piece in pieces:
        for copy in loads(*piece):
            copy.start()

    barrier = pltpu.get_barrier_semaphore()

    def greet_rep(d, carry):
        pl.semaphore_signal(barrier, inc=1, device_id={"rep": lax.rem(me + d, reps)})
        return carry

    def greet_grp(d, carry):
        pl.semaphore_signal(barrier, inc=1, device_id={"grp": lax.rem(my + d, grps)})
        return carry

    lax.fori_loop(1, reps, greet_rep, 0)
    lax.fori_loop(1, grps, greet_grp, 0)

    def to_peers(phase, axis, source, target):
        size, index = (reps, me) if axis == "rep" else (grps, my)
        send, recv = (rep_send, rep_recv) if axis == "rep" else (grp_send, grp_recv)

        def copy(d, at):
            peer = lax.rem(index + d, size)
            return pltpu.make_async_remote_copy(
                src_ref=source(peer),
                dst_ref=target.at[at],
                send_sem=send.at[phase, d],
                recv_sem=recv.at[phase, at],
                device_id={axis: peer},
            )

        def start(d, carry):
            copy(d, index).start()
            return carry

        def await_recv(d, carry):
            copy(d, lax.rem(index + d, size)).wait_recv()
            return carry

        def await_send(d, carry):
            copy(d, index).wait_send()
            return carry

        return (
            lambda: lax.fori_loop(1, size, start, 0),
            lambda: lax.fori_loop(1, size, await_recv, 0),
            lambda: lax.fori_loop(1, size, await_send, 0),
        )

    left_query = jnp.zeros((RANK, grad_query.shape[0]), F32)
    left_gate = left_query
    for start, size, index in pieces:
        for copy in loads(start, size, index):
            copy.wait()
        at = slice(start, start + size)
        high, low = split(grad_in[:, at] + error_in[:, at])
        merged_high[:, at] = high
        merged_low[:, at] = low
        if start < columns:
            basis = split(basis_query[:, at])
            left_query += three_pass(*basis, high, low, NT)
        else:
            basis = split(basis_gate[...])
            left_gate += three_pass(*basis, high, low, NT)

    length = vector_grad.shape[1]
    lines = -(-length // 128)
    own = jnp.concatenate([left_query, left_gate], axis=0)
    share = BOTH // reps
    left_send[...] = jnp.zeros_like(left_send)
    for i in range(reps):
        left_send[i, 0:share, :] = own[i * share : (i + 1) * share]
    for i in range(lines):
        width = min(128, length - i * 128)
        left_send[i, share : share + 1, 0:width] = vector_grad[:, i * 128 : i * 128 + width]

    pl.semaphore_wait(barrier, reps - 1 + grps - 1)

    start_1, recv_1, send_1 = to_peers(0, "rep", lambda peer: left_send.at[peer], left_recv)
    start_1()
    left_recv[me] = left_send[me]
    recv_1()
    total = left_recv[0]
    for i in range(1, reps):
        total += left_recv[i]
    left_sum[...] = total

    start_2, recv_2, send_2 = to_peers(1, "rep", lambda peer: left_sum, left_all)
    start_2()
    left_all[me] = total
    recv_2()
    for i in range(reps):
        left[i * share : (i + 1) * share, :] = left_all[i, 0:share, :]

    left_high, left_low = split(left[...])
    grams = []
    for part in (slice(0, RANK), slice(RANK, BOTH)):
        grams.append(
            three_pass(left_high[part], left_low[part], left_high[part], left_low[part], NT)
        )
    half = RANK // 2
    gram_all[my] = jnp.concatenate(
        [grams[0][:half], grams[0][half:], grams[1][:half], grams[1][half:]], axis=1
    )
    start_3, recv_3, send_3 = to_peers(0, "grp", lambda peer: gram_all.at[my], gram_all)
    start_3()

    vector_rows[...] = jnp.zeros_like(vector_rows)
    for i in range(lines):
        width = min(128, length - i * 128)
        at = slice(i * 128, i * 128 + width)
        mean = left_all[i, share : share + 1, 0:width] / reps
        new_momentum = 0.9 * vector_momentum[:, at] + mean
        new_master = vector_master[:, at] - 0.5 * new_momentum
        momentum_out[:, at] = new_momentum
        master_out[:, at] = new_master
        vector_rows[i : i + 1, 0:width] = new_master
    vector_send[...] = vector_rows[...].astype(BF16)
    start_v, recv_v, send_v = to_peers(1, "grp", lambda peer: vector_send, vector_all)
    start_v()
    vector_all[my] = vector_send[...]

    recv_3()
    gram = gram_all[0]
    for i in range(1, grps):
        gram += gram_all[i]
    quarters = [gram[:, i * RANK : (i + 1) * RANK] for i in range(4)]
    query_gram = jnp.concatenate(
        [quarters[0][:, 0:RANK], quarters[1][:, 0:RANK]], axis=0
    )
    gate_gram = jnp.concatenate([quarters[2], quarters[3]], axis=0)
    inverse = inverse_roots(query_gram, gate_gram)
    ortho = full_dot(inverse, left[...])
    ortho_out[...] = ortho
    ortho_high, ortho_low = split(ortho)

    rows = RANK // reps
    for start, size, index in pieces:
        at = slice(start, start + size)
        part = slice(0, RANK) if start < columns else slice(RANK, BOTH)
        terms = three_pass(
            ortho_high[part], ortho_low[part], merged_high[:, at], merged_low[:, at]
        )
        for i in range(reps):
            right_send[i, :, at] = terms[i * rows : (i + 1) * rows]
    start_4, recv_4, send_4 = to_peers(2, "rep", lambda peer: right_send.at[peer], right_recv)
    start_4()
    right_recv[me] = right_send[me]
    recv_4()
    total = right_recv[0]
    for i in range(1, reps):
        total += right_recv[i]

    right_part[my] = total
    start_5, recv_5, send_5 = to_peers(2, "grp", lambda peer: right_part.at[my], right_part)
    start_5()
    recv_5()
    total = right_part[0]
    for i in range(1, grps):
        total += right_part[i]
    right_final[...] = total

    start_6, recv_6, send_6 = to_peers(3, "rep", lambda peer: right_final, right_all)
    start_6()
    right_all[me] = total

    recv_v()
    low_lanes = lax.broadcasted_iota(jnp.int32, (lines - 1, 128), 1) < 64
    low_lane = lax.broadcasted_iota(jnp.int32, (1, 128), 1) < 64
    for i in range(grps // 2):
        base = i * 2 * length // 128
        even = vector_all[2 * i].astype(F32)
        odd = pltpu.roll(vector_all[2 * i + 1].astype(F32), 64, 1)
        vector_place[base : base + lines - 1, :] = even[: lines - 1]
        vector_place[base + lines - 1 : base + lines, :] = jnp.where(
            low_lane, even[lines - 1 : lines], odd[0:1]
        )
        vector_place[base + lines : base + 2 * lines - 1, :] = jnp.where(
            low_lanes, odd[: lines - 1], odd[1:lines]
        )
    weight_out[...] = vector_place[0 : weight_out.shape[0], :].astype(BF16)

    recv_6()
    for i in range(reps):
        right_out[i * rows : (i + 1) * rows, :] = right_all[i]
    for wait in (send_1, send_2, send_3, send_v, send_4, send_5, send_6):
        wait()


def finish_kernel(
    reps,
    ortho,
    right_query,
    right_gate,
    grad_query,
    error_query,
    momentum_query,
    master_query,
    grad_gate,
    error_gate,
    momentum_gate,
    master_gate,
    error_out_query,
    momentum_out_query,
    master_out_query,
    weight_out_query,
    error_out_gate,
    momentum_out_gate,
    master_out_gate,
    weight_out_gate,
    left_parts,
):
    @pl.when(pl.program_id(0) == 0)
    def _():
        for part, at in ((slice(0, RANK), 0), (slice(RANK, BOTH), 1)):
            high, low = split(ortho[part, :].T / reps)
            left_parts[at] = jnp.concatenate([high, high, low], axis=1)

    def update(index, right, grad, error, momentum, master, outs):
        high, low = split(right[...])
        approx = mm(left_parts[index], jnp.concatenate([high, low, high], axis=0))
        outs[0][...] = (grad[...] + error[...]) - approx
        new_momentum = 0.9 * momentum[...] + approx
        outs[1][...] = new_momentum
        new_master = master[...] - 0.5 * new_momentum
        outs[2][...] = new_master
        outs[3][...] = new_master.astype(BF16)

    update(
        0,
        right_query,
        grad_query,
        error_query,
        momentum_query,
        master_query,
        (error_out_query, momentum_out_query, master_out_query, weight_out_query),
    )

    @pl.when(pl.program_id(0) == 0)
    def _():
        update(
            1,
            right_gate,
            grad_gate,
            error_gate,
            momentum_gate,
            master_gate,
            (error_out_gate, momentum_out_gate, master_out_gate, weight_out_gate),
        )


def per_device(
    grad_query,
    error_query,
    basis_query,
    momentum_query,
    master_query,
    grad_gate,
    error_gate,
    basis_gate,
    momentum_gate,
    master_gate,
    vector_grad,
    vector_momentum,
    vector_master,
):
    reps, grps = lax.axis_size("rep"), lax.axis_size("grp")
    grad_query, error_query = grad_query[0], error_query[0]
    grad_gate, error_gate = grad_gate[0], error_gate[0]
    rows, columns = grad_query.shape
    gate = grad_gate.shape[1]
    both = columns + gate
    length = vector_grad.shape[1]
    share = RANK // reps
    any_spec = pl.BlockSpec(memory_space=pl.ANY)
    vmem_spec = pl.BlockSpec(memory_space=VMEM)
    ortho, right, vec_momentum, vec_master, vec_weight = pl.pallas_call(
        functools.partial(factor_kernel, reps, grps),
        out_shape=(
            jax.ShapeDtypeStruct((BOTH, rows), F32),
            jax.ShapeDtypeStruct((RANK, both), F32),
            jax.ShapeDtypeStruct((1, length), F32),
            jax.ShapeDtypeStruct((1, length), F32),
            jax.ShapeDtypeStruct((grps * length // 128, 128), BF16),
        ),
        in_specs=[
            any_spec,
            any_spec,
            vmem_spec,
            any_spec,
            any_spec,
            vmem_spec,
            vmem_spec,
            vmem_spec,
            vmem_spec,
        ],
        out_specs=[vmem_spec] * 5,
        scratch_shapes=[
            VMEM((rows, both), F32),
            VMEM((rows, both), F32),
            VMEM((rows, both), BF16),
            VMEM((rows, both), BF16),
            VMEM((reps, 8, rows), F32),
            VMEM((reps, 8, rows), F32),
            VMEM((8, rows), F32),
            VMEM((reps, 8, rows), F32),
            VMEM((BOTH, rows), F32),
            VMEM((grps, RANK // 2, 4 * RANK), F32),
            VMEM((16, 128), F32),
            VMEM((16, 128), BF16),
            VMEM((grps, 16, 128), BF16),
            VMEM((104, 128), F32),
            VMEM((reps, share, both), F32),
            VMEM((reps, share, both), F32),
            VMEM((grps, share, both), F32),
            VMEM((share, both), F32),
            VMEM((reps, share, both), F32),
            pltpu.SemaphoreType.DMA((2, columns // 512 + 1)),
            pltpu.SemaphoreType.DMA((4, reps)),
            pltpu.SemaphoreType.DMA((4, reps)),
            pltpu.SemaphoreType.DMA((3, grps)),
            pltpu.SemaphoreType.DMA((3, grps)),
        ],
        compiler_params=pltpu.CompilerParams(collective_id=0, has_side_effects=True),
        name="factors",
    )(
        grad_query,
        error_query,
        basis_query.T,
        grad_gate,
        error_gate,
        basis_gate.T,
        vector_grad,
        vector_momentum.reshape(1, length),
        vector_master.reshape(1, length),
    )

    tile = 256
    query_spec = pl.BlockSpec((rows, tile), lambda i: (0, i))
    gate_spec = pl.BlockSpec((rows, gate), lambda i: (0, 0))
    f32_query = jax.ShapeDtypeStruct((rows, columns), F32)
    f32_gate = jax.ShapeDtypeStruct((rows, gate), F32)
    outs = pl.pallas_call(
        functools.partial(finish_kernel, reps),
        grid=(columns // tile,),
        out_shape=(f32_query,) * 3
        + (jax.ShapeDtypeStruct((rows, columns), BF16),)
        + (f32_gate,) * 3
        + (jax.ShapeDtypeStruct((rows, gate), BF16),),
        in_specs=[
            pl.BlockSpec((BOTH, rows), lambda i: (0, 0)),
            pl.BlockSpec((RANK, tile), lambda i: (0, i)),
            pl.BlockSpec((RANK, gate), lambda i: (0, columns // gate)),
        ]
        + [query_spec] * 4
        + [gate_spec] * 4,
        out_specs=[query_spec] * 4 + [gate_spec] * 4,
        scratch_shapes=[VMEM((2, rows, 3 * RANK), BF16)],
        name="finish",
    )(
        ortho,
        right,
        right,
        grad_query,
        error_query,
        momentum_query,
        master_query,
        grad_gate,
        error_gate,
        momentum_gate,
        master_gate,
    )
    whole_query = lax.all_gather(outs[3], "grp", axis=0, tiled=True)
    whole_gate = lax.all_gather(outs[7], "grp", axis=0, tiled=True)
    return (
        outs[0][None],
        outs[1],
        outs[2],
        whole_query,
        right[:, :columns].T,
        outs[4][None],
        outs[5],
        outs[6],
        whole_gate,
        right[:, columns:].T,
        vec_momentum.reshape(length),
        vec_master.reshape(length),
        vec_weight.reshape(grps * length),
    )


def solution(mesh):
    in_specs = (
        P("rep", "grp", None),
        P("rep", "grp", None),
        P(),
        P("grp", None),
        P("grp", None),
        P("rep", "grp", None),
        P("rep", "grp", None),
        P(),
        P("grp", None),
        P("grp", None),
        P("rep", "grp"),
        P("grp"),
        P("grp"),
    )
    out_specs = (
        P("rep", "grp", None),
        P("grp", None),
        P("grp", None),
        P(),
        P(),
        P("rep", "grp", None),
        P("grp", None),
        P("grp", None),
        P(),
        P(),
        P("grp"),
        P("grp"),
        P(),
    )
    return jax.shard_map(
        per_device, mesh=mesh, in_specs=in_specs, out_specs=out_specs, check_vma=False
    )
```

time: 370 us -> 158 us (0.43)
  waiting for transfers between devices: 200 us -> 72.3 us
  blocking collectives: 111 us -> 0 us
  Pallas kernels: 0 us -> 55.5 us
  matrix products: 28.5 us -> 0 us
    psum x2 -> x0, waiting for transfers between devices: 157 us -> none  [the longest x1 83.3 us: per_device(): left_query, left_gate = lax.psum((local_query, local_gate), 'rep')]
    psum x2 -> x0, blocking collectives: 88.1 us -> none  [the longest x1 65.4 us: per_device(): lax.psum((terms_query, terms_gate), ('rep', 'grp'))]
    pallas_call x0 -> x2, Pallas kernels: none -> 55.5 us  [the longest x1 45.2 us: per_device(): pl.pallas_call(functools.partial(factor_kernel, reps, grps), out_shape=(j...]
    all_gather x2, waiting for transfers between devices: 42.8 us -> 71.6 us  [the longest x1 51.9 us: per_device(): whole_query = lax.all_gather(outs[3], 'grp', axis=0, tiled=True)]
    dot_general x32 -> x0, matrix products: 28.5 us -> none  [the longest x2 9.7 us: finish(): approx = jnp.dot(ortho, new_basis.T, precision=highest) / replicas]
    unnamed x1 -> x0, blocking collectives: 22.5 us -> none
    unnamed x36 -> x13, local copies, waits for them, and re-layouts: 11.1 us -> 10.1 us
  transfers between devices with their start and end apart: 4 -> 2, of which waited for: 3 -> 2; matrix products, arithmetic and copies ran while one was open for 3% -> 2% of each run, Pallas kernels for 0% -> 0%
where the time goes in v1:
time: 158 us; the launch traced here: 157 us
  waiting for transfers between devices  72.3 us (46%)
  Pallas kernels  55.5 us (35%)
  local copies, waits for them, and re-layouts  14.1 us (9%)
  between operations  14.1 us (9%)
    all_gather x1, waiting for transfers between devices, per_device(): whole_query = lax.all_gather(outs[3], 'grp', axis=0, tiled=True)  51.9 us
    pallas_call x1, Pallas kernels, per_device(): pl.pallas_call(functools.partial(factor_kernel, reps, grps), out_shape=(j...  45.2 us
    all_gather x1, waiting for transfers between devices, per_device(): whole_gate = lax.all_gather(outs[7], 'grp', axis=0, tiled=True)  19.7 us
    pallas_call x1, Pallas kernels, per_device(): pl.pallas_call(functools.partial(finish_kernel, reps), grid=(columns // t...  10.3 us
    unnamed x13, local copies, waits for them, and re-layouts  10.1 us
  transfers between devices with their start and end apart: 2, of which 2 were waited for; matrix products, arithmetic and copies ran while one was open for 2% of the time, Pallas kernels for 0%

profile of v1, /device:TPU:1, one launch (start us, length us, event | category | flops | bytes accessed | tf_op | source)
XLA Modules:
  0.0 157.3 jit_solution(17706230085821274373)
XLA Ops:
  7.2 0.0 all-gather.5.cloned.1.call-start
  7.2 1.3 reshape.41.vector_momentum
  8.5 1.3 reshape.42.vector_master
  9.8 45.2 %factors.1 = (f32[64,256]{1,0:T(8,128)}, f32[32,2304]{1,0:T(8,128)}, f32[1,1600]{1,0:T(1,128)}, f32[1,1600]{1,0:T(1,128)}, bf16[100,128]{1,0:T(8,128)(2,1)}) custom-call(f32[256,2048]{1,0:T(8,128)} %bitcast.13, f32[256,2048]{1,0:T(8,128)} %bitcast.15, f32[32,2048]{1,0:T(8,128)} %bitcast.21, f32[256,256]{1,0:T(8,128)} %bitcast.17, f32[256,256]{1,0:T(8,128)} %bitcast.19, ...), custom_call_target="tpu_custom_call" | custom-call | tf_op jit(solution)/shard_map/factors/pallas_call | solution.py:407
  55.0 0.0 copy-start.4
  55.0 0.0 copy-start.3
  55.0 0.0 copy-start
  55.1 10.3 %finish.1 = (f32[256,2048]{1,0:T(8,128)}, f32[256,2048]{1,0:T(8,128)}, f32[256,2048]{1,0:T(8,128)}, bf16[256,2048]{1,0:T(8,128)(2,1)}, f32[256,256]{1,0:T(8,128)...) custom-call(f32[64,256]{1,0:T(8,128)} %get-tuple-element.26.ortho, ...), custom_call_target="tpu_custom_call" | custom-call | tf_op jit(solution)/shard_map/finish/pallas_call | solution.py:473
  65.4 0.0 all-gather.5.cloned.1.call-update
  65.4 0.0 all-gather.3.cloned.1.call-start
  65.4 0.7 all-gather.3.cloned.1.call-update
  66.1 0.0 copy-done.4
  66.1 0.6 reduce
  66.8 0.0 copy-done.3
  66.8 0.6 reduce.1
  67.4 0.0 copy-done
  67.4 0.6 slice_bitcast_fusion.1
  68.0 0.7 slice_bitcast_fusion
  68.7 19.7 %all-gather.5.cloned.1.call-done = bf16[2048,256]{1,0:T(8,128)(2,1)} async-done(((bf16[256,256]{1,0:T(8,128)(2,1)}), bf16[2048,256]{1,0:T(8,128)(2,1)}) %all-gather.5.cloned.1.call-update) | async-done | bytes 1048592 | tf_op jit(solution)/shard_map/all_gather | solution.py:504
  88.5 51.9 %all-gather.3.cloned.1.call-done = bf16[2048,2048]{1,0:T(8,128)(2,1)} async-done(((bf16[256,2048]{1,0:T(8,128)(2,1)}), bf16[2048,2048]{1,0:T(8,128)(2,1)}) %all-gather.3.cloned.1.call-update) | async-done | bytes 8388624 | tf_op jit(solution)/shard_map/all_gather | solution.py:503
  140.3 0.0 copy-start.1
  140.3 8.5 %copy.29 = bf16[2048,2048]{1,0:T(8,128)(2,1)} copy(bf16[2048,2048]{1,0:T(8,128)(2,1)} %all-gather.3.cloned.1.call-done) | data formatting | bytes 16777216
  148.9 0.0 copy-done.1
  148.9 0.0 copy-start.2
  148.9 1.0 copy.30
  149.8 0.0 copy-done.2
  149.8 0.6 copy.31
Async XLA Ops:
  7.2 81.3 %all-gather.5.cloned.1.call-start = ((), (), s32[]{:S(2)}) async-start(), calls=%async_computation.1 | async-start | bytes 1179648 | tf_op jit(solution)/shard_map/all_gather | solution.py:504
  55.0 11.1 %copy-start.4 = (f32[1,1600]{1,0:T(1,128)S(1)}, f32[1,1600]{1,0:T(1,128)}, u32[]{:S(2)}) copy-start(f32[1,1600]{1,0:T(1,128)} %get-tuple-element.36) | copy-start | bytes 19204
  55.0 11.7 %copy-start.3 = (f32[1,1600]{1,0:T(1,128)S(1)}, f32[1,1600]{1,0:T(1,128)}, u32[]{:S(2)}) copy-start(f32[1,1600]{1,0:T(1,128)} %get-tuple-element.37) | copy-start | bytes 19204
  55.0 12.3 %copy-start = (f32[32,2304]{1,0:T(8,128)S(1)}, f32[32,2304]{1,0:T(8,128)}, u32[]{:S(2)}) copy-start(f32[32,2304]{1,0:T(8,128)} %get-tuple-element.27.right_query.right_gate) | copy-start | bytes 884740
  65.4 75.0 %all-gather.3.cloned.1.call-start = ((), (), s32[]{:S(2)}) async-start(), calls=%async_computation | async-start | bytes 9437184 | tf_op jit(solution)/shard_map/all_gather | solution.py:503
  140.3 8.5 %copy-start.1 = (bf16[2048,256]{1,0:T(8,128)(2,1)S(1)}, bf16[2048,256]{1,0:T(8,128)(2,1)}, u32[]{:S(2)}) copy-start(bf16[2048,256]{1,0:T(8,128)(2,1)} %all-gather.5.cloned.1.call-done) | copy-start | bytes 3145732
  148.9 1.0 copy-start.2
Sparse Core Ops, SparseCore 0:
  65.5 22.9 all-gather.4
  90.7 49.5 all-gather.2

commit v2 on v1

--- a/solution.py
+++ b/solution.py
@@ -75,13 +75,22 @@
     vector_grad,
     vector_momentum,
     vector_master,
-    ortho_out,
+    momentum_query,
+    master_query,
+    momentum_gate,
+    master_gate,
     right_out,
     momentum_out,
     master_out,
     weight_out,
+    new_error,
+    new_momentum,
+    new_master,
+    weights,
     grad_in,
     error_in,
+    momentum_in,
+    master_in,
     merged_high,
     merged_low,
     left_send,
@@ -104,6 +113,12 @@
     rep_recv,
     grp_send,
     grp_recv,
+    x_send,
+    x_recv,
+    plane_send,
+    plane_recv,
+    core_send,
+    core_recv,
 ):
     me = lax.axis_index("rep")
     my = lax.axis_index("grp")
@@ -131,6 +146,19 @@
     for piece in pieces:
         for copy in loads(*piece):
             copy.start()
+
+    later = [
+        pltpu.make_async_copy(source, into.at[:, at], load_sem.at[2 + i, j])
+        for i, (into, pair) in enumerate(
+            (
+                (momentum_in, (momentum_query, momentum_gate)),
+                (master_in, (master_query, master_gate)),
+            )
+        )
+        for j, (source, at) in enumerate(zip(pair, (pl.ds(0, columns), pl.ds(columns, gate))))
+    ]
+    for copy in later:
+        copy.start()
 
     barrier = pltpu.get_barrier_semaphore()
 
@@ -240,11 +268,11 @@
         width = min(128, length - i * 128)
         at = slice(i * 128, i * 128 + width)
         mean = left_all[i, share : share + 1, 0:width] / reps
-        new_momentum = 0.9 * vector_momentum[:, at] + mean
-        new_master = vector_master[:, at] - 0.5 * new_momentum
-        momentum_out[:, at] = new_momentum
-        master_out[:, at] = new_master
-        vector_rows[i : i + 1, 0:width] = new_master
+        gain_momentum = 0.9 * vector_momentum[:, at] + mean
+        gain = vector_master[:, at] - 0.5 * gain_momentum
+        momentum_out[:, at] = gain_momentum
+        master_out[:, at] = gain
+        vector_rows[i : i + 1, 0:width] = gain
     vector_send[...] = vector_rows[...].astype(BF16)
     start_v, recv_v, send_v = to_peers(1, "grp", lambda peer: vector_send, vector_all)
     start_v()
@@ -261,7 +289,6 @@
     gate_gram = jnp.concatenate([quarters[2], quarters[3]], axis=0)
     inverse = inverse_roots(query_gram, gate_gram)
     ortho = full_dot(inverse, left[...])
-    ortho_out[...] = ortho
     ortho_high, ortho_low = split(ortho)
 
     rows = RANK // reps
@@ -313,70 +340,124 @@
     recv_6()
     for i in range(reps):
         right_out[i * rows : (i + 1) * rows, :] = right_all[i]
+
+    for copy in later:
+        copy.wait()
+    block = grad_query.shape[0]
+    factors = []
+    for part in (slice(0, RANK), slice(RANK, BOTH)):
+        high, low = split(ortho[part].T / reps)
+        factors.append(jnp.concatenate([high, high, low], axis=1))
+    own_rows = pl.ds(pl.multiple_of(my * block, block), block)
+    tiles = [(start, 256) for start in range(0, columns + gate, 256)]
+    for start, size in tiles:
+        at = slice(start, start + size)
+        high, low = split(right_out[:, at])
+        approx = mm(
+            factors[0 if start < columns else 1],
+            jnp.concatenate([high, low, high], axis=0),
+        )
+        new_error[:, at] = approx
+        moved = 0.9 * momentum_in[:, at] + approx
+        new_momentum[:, at] = moved
+        updated = master_in[:, at] - 0.5 * moved
+        new_master[:, at] = updated
+        weights[own_rows, at] = updated.astype(BF16)
+
+    side = 4
+    y, z, x, core = me // side, me % side, my // 2, my % 2
+    half = block // 2
+    strip = half // side
+    offsets = (1, 3, 2)
+
+    def move(row, size, send, recv, **peer):
+        place = weights.at[pl.ds(pl.multiple_of(row, strip), size)]
+        return pltpu.make_async_remote_copy(
+            src_ref=place, dst_ref=place, send_sem=send, recv_sem=recv, device_id=peer
+        )
+
+    def strip_row(block_index, part, at):
+        return block_index * block + part * half + at * strip
+
+    def along_x(k, part, from_x):
+        return move(
+            strip_row(from_x * 2 + core, part, (y, z)[part]),
+            strip,
+            x_send.at[k, part],
+            x_recv.at[k, part],
+            grp=lax.rem(x + k, side) * 2 + core,
+        )
+
+    def in_plane(k, part, j, at):
+        from_x = lax.rem(x - k + side, side)
+        peer = (
+            lax.rem(y + j, side) * side + z if part == 0 else y * side + lax.rem(z + j, side)
+        )
+        return move(
+            strip_row(from_x * 2 + core, part, at),
+            strip,
+            plane_send.at[k, part, j],
+            plane_recv.at[k, part, j],
+            rep=peer,
+        )
+
+    def to_core(k, part, from_core):
+        from_x = lax.rem(x - k + side, side)
+        return move(
+            strip_row(from_x * 2 + from_core, part, 0),
+            half,
+            core_send.at[k, part],
+            core_recv.at[k, part],
+            grp=x * 2 + 1 - core,
+        )
+
+    for k in offsets:
+        for part in (0, 1):
+            along_x(k, part, x).start()
+    for part in (0, 1):
+        to_core(0, part, core).start()
+    for start, size in tiles:
+        at = slice(start, start + size)
+        new_error[:, at] = (grad_in[:, at] + error_in[:, at]) - new_error[:, at]
+    for k in offsets:
+        for part in (0, 1):
+            along_x(k, part, lax.rem(x - k + side, side)).wait_recv()
+            for j in offsets:
+                in_plane(k, part, j, (y, z)[part]).start()
+    for k in offsets:
+        for part in (0, 1):
+            for j in offsets:
+                at = lax.rem((y, z)[part] - j + side, side)
+                in_plane(k, part, j, at).wait_recv()
+            to_core(k, part, core).start()
+    for k in (0,) + offsets:
+        for part in (0, 1):
+            to_core(k, part, 1 - core).wait_recv()
+            to_core(k, part, core).wait_send()
+    for k in offsets:
+        for part in (0, 1):
+            along_x(k, part, x).wait_send()
+            for j in offsets:
+                in_plane(k, part, j, (y, z)[part]).wait_send()
     for wait in (send_1, send_2, send_3, send_v, send_4, send_5, send_6):
         wait()
 
 
-def finish_kernel(
-    reps,
-    ortho,
-    right_query,
-    right_gate,
-    grad_query,
-    error_query,
-    momentum_query,
-    master_query,
-    grad_gate,
-    error_gate,
-    momentum_gate,
-    master_gate,
-    error_out_query,
-    momentum_out_query,
-    master_out_query,
-    weight_out_query,
-    error_out_gate,
-    momentum_out_gate,
-    master_out_gate,
-    weight_out_gate,
-    left_parts,
-):
-    @pl.when(pl.program_id(0) == 0)
-    def _():
-        for part, at in ((slice(0, RANK), 0), (slice(RANK, BOTH), 1)):
-            high, low = split(ortho[part, :].T / reps)
-            left_parts[at] = jnp.concatenate([high, high, low], axis=1)
-
-    def update(index, right, grad, error, momentum, master, outs):
-        high, low = split(right[...])
-        approx = mm(left_parts[index], jnp.concatenate([high, low, high], axis=0))
-        outs[0][...] = (grad[...] + error[...]) - approx
-        new_momentum = 0.9 * momentum[...] + approx
-        outs[1][...] = new_momentum
-        new_master = master[...] - 0.5 * new_momentum
-        outs[2][...] = new_master
-        outs[3][...] = new_master.astype(BF16)
-
-    update(
-        0,
-        right_query,
-        grad_query,
-        error_query,
-        momentum_query,
-        master_query,
-        (error_out_query, momentum_out_query, master_out_query, weight_out_query),
-    )
-
-    @pl.when(pl.program_id(0) == 0)
-    def _():
-        update(
-            1,
-            right_gate,
-            grad_gate,
-            error_gate,
-            momentum_gate,
-            master_gate,
-            (error_out_gate, momentum_out_gate, master_out_gate, weight_out_gate),
-        )
+def write_kernel(columns, *refs):
+    right, momentum, master, gains, error, new_momentum, new_master, weights = refs[:8]
+    outs, sems = refs[8:-1], refs[-1]
+    query, gate = pl.ds(0, columns), pl.ds(columns, right.shape[1] - columns)
+    sources = []
+    for whole in (weights, error, new_momentum, new_master, right):
+        sources += [whole.at[:, query], whole.at[:, gate]]
+    copies = [
+        pltpu.make_async_copy(source, out, sems.at[i])
+        for i, (source, out) in enumerate(zip(sources + [momentum, master, gains], outs))
+    ]
+    for copy in copies:
+        copy.start()
+    for copy in copies:
+        copy.wait()
 
 
 def per_device(
@@ -404,15 +485,19 @@
     share = RANK // reps
     any_spec = pl.BlockSpec(memory_space=pl.ANY)
     vmem_spec = pl.BlockSpec(memory_space=VMEM)
-    ortho, right, vec_momentum, vec_master, vec_weight = pl.pallas_call(
+    held = (
+        ((RANK, both), F32),
+        ((1, length), F32),
+        ((1, length), F32),
+        ((grps * length // 128, 128), BF16),
+        ((rows, both), F32),
+        ((rows, both), F32),
+        ((rows, both), F32),
+        ((grps * rows, both), BF16),
+    )
+    parts = pl.pallas_call(
         functools.partial(factor_kernel, reps, grps),
-        out_shape=(
-            jax.ShapeDtypeStruct((BOTH, rows), F32),
-            jax.ShapeDtypeStruct((RANK, both), F32),
-            jax.ShapeDtypeStruct((1, length), F32),
-            jax.ShapeDtypeStruct((1, length), F32),
-            jax.ShapeDtypeStruct((grps * length // 128, 128), BF16),
-        ),
+        out_shape=tuple(VMEM(*entry) for entry in held),
         in_specs=[
             any_spec,
             any_spec,
@@ -423,9 +508,15 @@
             vmem_spec,
             vmem_spec,
             vmem_spec,
+            any_spec,
+            any_spec,
+            any_spec,
+            any_spec,
         ],
-        out_specs=[vmem_spec] * 5,
+        out_specs=[vmem_spec] * len(held),
         scratch_shapes=[
+            VMEM((rows, both), F32),
+            VMEM((rows, both), F32),
             VMEM((rows, both), F32),
             VMEM((rows, both), F32),
             VMEM((rows, both), BF16),
@@ -445,13 +536,21 @@
             VMEM((grps, share, both), F32),
             VMEM((share, both), F32),
             VMEM((reps, share, both), F32),
-            pltpu.SemaphoreType.DMA((2, columns // 512 + 1)),
+            pltpu.SemaphoreType.DMA((4, columns // 512 + 1)),
             pltpu.SemaphoreType.DMA((4, reps)),
             pltpu.SemaphoreType.DMA((4, reps)),
             pltpu.SemaphoreType.DMA((3, grps)),
             pltpu.SemaphoreType.DMA((3, grps)),
+            pltpu.SemaphoreType.DMA((4, 2)),
+            pltpu.SemaphoreType.DMA((4, 2)),
+            pltpu.SemaphoreType.DMA((4, 2, 4)),
+            pltpu.SemaphoreType.DMA((4, 2, 4)),
+            pltpu.SemaphoreType.DMA((4, 2)),
+            pltpu.SemaphoreType.DMA((4, 2)),
         ],
-        compiler_params=pltpu.CompilerParams(collective_id=0, has_side_effects=True),
+        compiler_params=pltpu.CompilerParams(
+            collective_id=0, has_side_effects=True, vmem_limit_bytes=40 << 20
+        ),
         name="factors",
     )(
         grad_query,
@@ -463,59 +562,44 @@
         vector_grad,
         vector_momentum.reshape(1, length),
         vector_master.reshape(1, length),
-    )
-
-    tile = 256
-    query_spec = pl.BlockSpec((rows, tile), lambda i: (0, i))
-    gate_spec = pl.BlockSpec((rows, gate), lambda i: (0, 0))
-    f32_query = jax.ShapeDtypeStruct((rows, columns), F32)
-    f32_gate = jax.ShapeDtypeStruct((rows, gate), F32)
-    outs = pl.pallas_call(
-        functools.partial(finish_kernel, reps),
-        grid=(columns // tile,),
-        out_shape=(f32_query,) * 3
-        + (jax.ShapeDtypeStruct((rows, columns), BF16),)
-        + (f32_gate,) * 3
-        + (jax.ShapeDtypeStruct((rows, gate), BF16),),
-        in_specs=[
-            pl.BlockSpec((BOTH, rows), lambda i: (0, 0)),
-            pl.BlockSpec((RANK, tile), lambda i: (0, i)),
-            pl.BlockSpec((RANK, gate), lambda i: (0, columns // gate)),
-        ]
-        + [query_spec] * 4
-        + [gate_spec] * 4,
-        out_specs=[query_spec] * 4 + [gate_spec] * 4,
-        scratch_shapes=[VMEM((2, rows, 3 * RANK), BF16)],
-        name="finish",
-    )(
-        ortho,
-        right,
-        right,
-        grad_query,
-        error_query,
         momentum_query,
         master_query,
-        grad_gate,
-        error_gate,
         momentum_gate,
         master_gate,
     )
-    whole_query = lax.all_gather(outs[3], "grp", axis=0, tiled=True)
-    whole_gate = lax.all_gather(outs[7], "grp", axis=0, tiled=True)
+
+    def shapes(row_count, dtype):
+        return [
+            jax.ShapeDtypeStruct((row_count, columns), dtype),
+            jax.ShapeDtypeStruct((row_count, gate), dtype),
+        ]
+
+    outs = pl.pallas_call(
+        functools.partial(write_kernel, columns),
+        out_shape=shapes(grps * rows, BF16)
+        + shapes(rows, F32) * 3
+        + shapes(RANK, F32)
+        + [jax.ShapeDtypeStruct(*entry) for entry in held[1:4]],
+        in_specs=[vmem_spec] * len(held),
+        out_specs=[any_spec] * 13,
+        scratch_shapes=[pltpu.SemaphoreType.DMA((13,))],
+        compiler_params=pltpu.CompilerParams(vmem_limit_bytes=8 << 20),
+        name="write",
+    )(*parts)
     return (
-        outs[0][None],
+        outs[2][None],
+        outs[4],
+        outs[6],
+        outs[0],
+        outs[8].T,
+        outs[3][None],
+        outs[5],
+        outs[7],
         outs[1],
-        outs[2],
-        whole_query,
-        right[:, :columns].T,
-        outs[4][None],
-        outs[5],
-        outs[6],
-        whole_gate,
-        right[:, columns:].T,
-        vec_momentum.reshape(length),
-        vec_master.reshape(length),
-        vec_weight.reshape(grps * length),
+        outs[9].T,
+        outs[10].reshape(length),
+        outs[11].reshape(length),
+        outs[12].reshape(grps * length),
     )
 
 

time: 158 us -> 89.5 us (0.57)
  waiting for transfers between devices: 72.3 us -> 0 us
  Pallas kernels: 55.5 us -> 84.8 us
  between operations: 14.1 us -> 0.66 us
  local copies, waits for them, and re-layouts: 14.1 us -> 2.59 us
    all_gather x2 -> x0, waiting for transfers between devices: 71.6 us -> none  [the longest x1 51.9 us: per_device(): whole_query = lax.all_gather(outs[3], 'grp', axis=0, tiled=True)]
    pallas_call x2, Pallas kernels: 55.5 us -> 84.8 us  [the longest x1 78.8 us: per_device(): pl.pallas_call(functools.partial(factor_kernel, reps, grps), out_shape=tu...]
    unnamed x13 -> x0, local copies, waits for them, and re-layouts: 10.1 us -> none
  transfers between devices with their start and end apart: 2 -> 0, of which waited for: 2 -> 0; matrix products, arithmetic and copies ran while one was open for 2% -> 0% of each run, Pallas kernels for 0% -> 0%
where the time goes in v2:
time: 89.5 us; the launch traced here: 89.3 us
  Pallas kernels  84.8 us (95%)
  local copies, waits for them, and re-layouts  2.59 us (3%)
  other arithmetic  1.24 us (1%)
    pallas_call x1, Pallas kernels, per_device(): pl.pallas_call(functools.partial(factor_kernel, reps, grps), out_shape=tu...  78.8 us
    pallas_call x1, Pallas kernels, per_device(): pl.pallas_call(functools.partial(write_kernel, columns), out_shape=shapes...  6.04 us

profile of v2, /device:TPU:1, one launch (start us, length us, event | category | flops | bytes accessed | tf_op | source)
XLA Modules:
  0.0 89.3 jit_solution(13780693304657348648)
XLA Ops:
  0.6 1.3 %reshape.41.vector_momentum = f32[1,1600]{1,0:T(1,128)} reshape(f32[1600]{0:T(1024)} %param.24) | data formatting | bytes 12800 | tf_op jit(solution)/shard_map/reshape | solution.py:563
  1.9 1.3 %reshape.42.vector_master = f32[1,1600]{1,0:T(1,128)} reshape(f32[1600]{0:T(1024)} %param.25) | data formatting | bytes 12800 | tf_op jit(solution)/shard_map/reshape | solution.py:564
  3.2 78.8 %factors.1 = (f32[32,2304]{1,0:T(8,128)S(1)}, f32[1,1600]{1,0:T(1,128)S(1)}, f32[1,1600]{1,0:T(1,128)S(1)}, bf16[100,128]{1,0:T(8,128)(2,1)S(1)}, f32[256,2304]{...) custom-call(f32[256,2048]{1,0:T(8,128)} %bitcast.11, ...), custom_call_target="tpu_custom_call" | custom-call | tf_op jit(solution)/shard_map/factors/pallas_call | solution.py:498
  82.0 6.0 %write.1 = (bf16[2048,2048]{1,0:T(8,128)(2,1)}, bf16[2048,256]{1,0:T(8,128)(2,1)}, f32[256,2048]{1,0:T(8,128)}, f32[256,256]{1,0:T(8,128)}, f32[256,2048]{1,0:T(...) custom-call(f32[32,2304]{1,0:T(8,128)S(1)} %get-tuple-element.34.ref, ...), custom_call_target="tpu_custom_call" | custom-call | tf_op jit(solution)/shard_map/write/pallas_call | solution.py:577
  88.1 0.6 reduce
  88.7 0.6 reduce.1

commit v3 on v2

--- a/solution.py
+++ b/solution.py
@@ -108,6 +108,9 @@
     right_part,
     right_final,
     right_all,
+    basis_in,
+    vector_in,
+    first_sem,
     load_sem,
     rep_send,
     rep_recv,
@@ -143,6 +146,13 @@
             ),
         )
 
+    first = [
+        pltpu.make_async_copy(basis_query, basis_in.at[:, pl.ds(0, columns)], first_sem.at[0]),
+        pltpu.make_async_copy(basis_gate, basis_in.at[:, pl.ds(columns, gate)], first_sem.at[1]),
+        pltpu.make_async_copy(vector_grad, vector_in, first_sem.at[2]),
+    ]
+    for copy in first:
+        copy.start()
     for piece in pieces:
         for copy in loads(*piece):
             copy.start()
@@ -157,9 +167,6 @@
         )
         for j, (source, at) in enumerate(zip(pair, (pl.ds(0, columns), pl.ds(columns, gate))))
     ]
-    for copy in later:
-        copy.start()
-
     barrier = pltpu.get_barrier_semaphore()
 
     def greet_rep(d, carry):
@@ -205,6 +212,8 @@
             lambda: lax.fori_loop(1, size, await_send, 0),
         )
 
+    for copy in first:
+        copy.wait()
     left_query = jnp.zeros((RANK, grad_query.shape[0]), F32)
     left_gate = left_query
     for start, size, index in pieces:
@@ -215,12 +224,14 @@
         merged_high[:, at] = high
         merged_low[:, at] = low
         if start < columns:
-            basis = split(basis_query[:, at])
+            basis = split(basis_in[:, at])
             left_query += three_pass(*basis, high, low, NT)
         else:
-            basis = split(basis_gate[...])
+            basis = split(basis_in[:, at])
             left_gate += three_pass(*basis, high, low, NT)
 
+    for copy in later:
+        copy.start()
     length = vector_grad.shape[1]
     lines = -(-length // 128)
     own = jnp.concatenate([left_query, left_gate], axis=0)
@@ -230,7 +241,7 @@
         left_send[i, 0:share, :] = own[i * share : (i + 1) * share]
     for i in range(lines):
         width = min(128, length - i * 128)
-        left_send[i, share : share + 1, 0:width] = vector_grad[:, i * 128 : i * 128 + width]
+        left_send[i, share : share + 1, 0:width] = vector_in[:, i * 128 : i * 128 + width]
 
     pl.semaphore_wait(barrier, reps - 1 + grps - 1)
 
@@ -268,10 +279,10 @@
         width = min(128, length - i * 128)
         at = slice(i * 128, i * 128 + width)
         mean = left_all[i, share : share + 1, 0:width] / reps
-        gain_momentum = 0.9 * vector_momentum[:, at] + mean
-        gain = vector_master[:, at] - 0.5 * gain_momentum
-        momentum_out[:, at] = gain_momentum
-        master_out[:, at] = gain
+        gain_momentum = 0.9 * vector_momentum[at].reshape(1, width) + mean
+        gain = vector_master[at].reshape(1, width) - 0.5 * gain_momentum
+        momentum_out[at] = gain_momentum.reshape(width)
+        master_out[at] = gain.reshape(width)
         vector_rows[i : i + 1, 0:width] = gain
     vector_send[...] = vector_rows[...].astype(BF16)
     start_v, recv_v, send_v = to_peers(1, "grp", lambda peer: vector_send, vector_all)
@@ -368,77 +379,122 @@
     y, z, x, core = me // side, me % side, my // 2, my % 2
     half = block // 2
     strip = half // side
-    offsets = (1, 3, 2)
 
     def move(row, size, send, recv, **peer):
-        place = weights.at[pl.ds(pl.multiple_of(row, strip), size)]
+        span = weights.at[pl.ds(pl.multiple_of(row, strip // 2), size)]
         return pltpu.make_async_remote_copy(
-            src_ref=place, dst_ref=place, send_sem=send, recv_sem=recv, device_id=peer
-        )
-
-    def strip_row(block_index, part, at):
-        return block_index * block + part * half + at * strip
-
-    def along_x(k, part, from_x):
+            src_ref=span, dst_ref=span, send_sem=send, recv_sem=recv, device_id=peer
+        )
+
+    def rows_of(from_x, from_core, part, at):
+        return (from_x * 2 + from_core) * block + part * half + at * strip
+
+    def wrap(value):
+        return lax.rem(value + 2 * side, side)
+
+    place = (y, z)
+
+    def along_x(k, part, from_x, hop):
         return move(
-            strip_row(from_x * 2 + core, part, (y, z)[part]),
+            rows_of(from_x, core, part, place[part]),
             strip,
             x_send.at[k, part],
             x_recv.at[k, part],
-            grp=lax.rem(x + k, side) * 2 + core,
-        )
-
-    def in_plane(k, part, j, at):
-        from_x = lax.rem(x - k + side, side)
+            grp=wrap(x + hop) * 2 + core,
+        )
+
+    def in_plane(k, part, j, hop):
+        offset = {1: 0, 3: 0, 2: -hop, 0: -hop}[j]
+        return strip_move(k, part, j, offset, hop)
+
+    def strip_move(k, part, j, offset, hop):
+        row = rows_of(wrap(x - k), core, part, wrap(place[part] + offset))
+        size = strip if j in (1, 3) else strip // 2
+        if j == 0:
+            row += strip // 2
         peer = (
-            lax.rem(y + j, side) * side + z if part == 0 else y * side + lax.rem(z + j, side)
+            wrap(y + hop) * side + z if part == 0 else y * side + wrap(z + hop)
         )
         return move(
-            strip_row(from_x * 2 + core, part, at),
-            strip,
-            plane_send.at[k, part, j],
-            plane_recv.at[k, part, j],
-            rep=peer,
-        )
-
-    def to_core(k, part, from_core):
-        from_x = lax.rem(x - k + side, side)
+            row, size, plane_send.at[k, part, j], plane_recv.at[k, part, j], rep=peer
+        )
+
+    landed = {1: -1, 3: 1, 2: -2, 0: -2}
+
+    def to_core(k, part, j, from_core):
+        row = rows_of(
+            wrap(x - k), from_core, part, wrap(place[part] + landed.get(j, 0))
+        )
+        if j == 0:
+            row += strip // 2
         return move(
-            strip_row(from_x * 2 + from_core, part, 0),
+            row,
+            strip // 2 if j in (0, 2) else strip,
+            core_send.at[k, part, j],
+            core_recv.at[k, part, j],
+            grp=x * 2 + 1 - core,
+        )
+
+    def own_to_core(part, from_core):
+        return move(
+            rows_of(x, from_core, part, 0),
             half,
-            core_send.at[k, part],
-            core_recv.at[k, part],
+            core_send.at[0, part, 0],
+            core_recv.at[0, part, 0],
             grp=x * 2 + 1 - core,
         )
 
-    for k in offsets:
-        for part in (0, 1):
-            along_x(k, part, x).start()
-    for part in (0, 1):
-        to_core(0, part, core).start()
+    sends = [along_x(1, 0, x, 1), along_x(3, 1, x, 3), along_x(1, 1, x, 1), along_x(3, 0, x, 3)]
+    sends += [own_to_core(0, core), own_to_core(1, core)]
+    for copy in sends:
+        copy.start()
     for start, size in tiles:
         at = slice(start, start + size)
         new_error[:, at] = (grad_in[:, at] + error_in[:, at]) - new_error[:, at]
-    for k in offsets:
+
+    def begin(*copies):
+        for copy in copies:
+            copy.start()
+            sends.append(copy)
+
+    def from_x(k, part):
+        along_x(k, part, wrap(x - k), 0).wait_recv()
+        if (k, part) in ((1, 0), (3, 1)):
+            begin(along_x(2, part, wrap(x - k), k))
+        begin(
+            in_plane(k, part, 1, 1), in_plane(k, part, 3, 3), to_core(k, part, 4, core)
+        )
+
+    def from_neighbours(k, part):
+        for j, relayed in ((1, 2), (3, 0)):
+            strip_move(k, part, j, landed[j], j).wait_recv()
+            begin(in_plane(k, part, relayed, j), to_core(k, part, j, core))
+
+    def from_opposite(k, part):
+        for j in (2, 0):
+            strip_move(k, part, j, landed[j], 1).wait_recv()
+            begin(to_core(k, part, j, core))
+
+    for k, part in ((1, 0), (3, 1), (3, 0), (1, 1)):
+        from_x(k, part)
+    for k, part in ((1, 0), (3, 1), (3, 0), (1, 1)):
+        from_neighbours(k, part)
+    for part in (0, 1):
+        from_x(2, part)
+    for k, part in ((1, 0), (3, 1), (3, 0), (1, 1)):
+        from_opposite(k, part)
+    for part in (0, 1):
+        from_neighbours(2, part)
+    for part in (0, 1):
+        from_opposite(2, part)
+    for part in (0, 1):
+        own_to_core(part, 1 - core).wait_recv()
+    for k in (1, 3, 2):
         for part in (0, 1):
-            along_x(k, part, lax.rem(x - k + side, side)).wait_recv()
-            for j in offsets:
-                in_plane(k, part, j, (y, z)[part]).start()
-    for k in offsets:
-        for part in (0, 1):
-            for j in offsets:
-                at = lax.rem((y, z)[part] - j + side, side)
-                in_plane(k, part, j, at).wait_recv()
-            to_core(k, part, core).start()
-    for k in (0,) + offsets:
-        for part in (0, 1):
-            to_core(k, part, 1 - core).wait_recv()
-            to_core(k, part, core).wait_send()
-    for k in offsets:
-        for part in (0, 1):
-            along_x(k, part, x).wait_send()
-            for j in offsets:
-                in_plane(k, part, j, (y, z)[part]).wait_send()
+            for j in range(5):
+                to_core(k, part, j, 1 - core).wait_recv()
+    for copy in sends:
+        copy.wait_send()
     for wait in (send_1, send_2, send_3, send_v, send_4, send_5, send_6):
         wait()
 
@@ -487,8 +543,8 @@
     vmem_spec = pl.BlockSpec(memory_space=VMEM)
     held = (
         ((RANK, both), F32),
-        ((1, length), F32),
-        ((1, length), F32),
+        ((length,), F32),
+        ((length,), F32),
         ((grps * length // 128, 128), BF16),
         ((rows, both), F32),
         ((rows, both), F32),
@@ -498,21 +554,7 @@
     parts = pl.pallas_call(
         functools.partial(factor_kernel, reps, grps),
         out_shape=tuple(VMEM(*entry) for entry in held),
-        in_specs=[
-            any_spec,
-            any_spec,
-            vmem_spec,
-            any_spec,
-            any_spec,
-            vmem_spec,
-            vmem_spec,
-            vmem_spec,
-            vmem_spec,
-            any_spec,
-            any_spec,
-            any_spec,
-            any_spec,
-        ],
+        in_specs=[any_spec] * 7 + [vmem_spec] * 2 + [any_spec] * 4,
         out_specs=[vmem_spec] * len(held),
         scratch_shapes=[
             VMEM((rows, both), F32),
@@ -536,6 +578,9 @@
             VMEM((grps, share, both), F32),
             VMEM((share, both), F32),
             VMEM((reps, share, both), F32),
+            VMEM((RANK, both), F32),
+            VMEM((1, length), F32),
+            pltpu.SemaphoreType.DMA((3,)),
             pltpu.SemaphoreType.DMA((4, columns // 512 + 1)),
             pltpu.SemaphoreType.DMA((4, reps)),
             pltpu.SemaphoreType.DMA((4, reps)),
@@ -545,8 +590,8 @@
             pltpu.SemaphoreType.DMA((4, 2)),
             pltpu.SemaphoreType.DMA((4, 2, 4)),
             pltpu.SemaphoreType.DMA((4, 2, 4)),
-            pltpu.SemaphoreType.DMA((4, 2)),
-            pltpu.SemaphoreType.DMA((4, 2)),
+            pltpu.SemaphoreType.DMA((4, 2, 5)),
+            pltpu.SemaphoreType.DMA((4, 2, 5)),
         ],
         compiler_params=pltpu.CompilerParams(
             collective_id=0, has_side_effects=True, vmem_limit_bytes=40 << 20
@@ -560,8 +605,8 @@
         error_gate,
         basis_gate.T,
         vector_grad,
-        vector_momentum.reshape(1, length),
-        vector_master.reshape(1, length),
+        vector_momentum,
+        vector_master,
         momentum_query,
         master_query,
         momentum_gate,
@@ -597,8 +642,8 @@
         outs[7],
         outs[1],
         outs[9].T,
-        outs[10].reshape(length),
-        outs[11].reshape(length),
+        outs[10],
+        outs[11],
         outs[12].reshape(grps * length),
     )
 

time: 89.5 us -> 82.4 us (0.921)
  Pallas kernels: 84.8 us -> 81.6 us
  local copies, waits for them, and re-layouts: 2.59 us -> 0 us
  other arithmetic: 1.24 us -> 0 us
    pallas_call x1, Pallas kernels: 78.8 us -> 75.5 us  [per_device(): pl.pallas_call(functools.partial(factor_kernel, reps, grps), out_shape=tu...]
    reshape x2 -> x0, local copies, waits for them, and re-layouts: 2.59 us -> none  [the longest x1 1.3 us: per_device(): vector_momentum.reshape(1, length)]
    pallas_call x2 -> x0, other arithmetic: 1.24 us -> none  [per_device(): pl.pallas_call(functools.partial(write_kernel, columns), out_shape=shapes...]
where the time goes in v3:
time: 82.4 us; the launch traced here: 82.2 us
  Pallas kernels  81.6 us (99%)
    pallas_call x1, Pallas kernels, per_device(): pl.pallas_call(functools.partial(factor_kernel, reps, grps), out_shape=tu...  75.5 us
    pallas_call x1, Pallas kernels, per_device(): pl.pallas_call(functools.partial(write_kernel, columns), out_shape=shapes...  6.04 us

profile of v3, /device:TPU:1, one launch (start us, length us, event | category | flops | bytes accessed | tf_op | source)
XLA Modules:
  0.0 82.2 jit_solution(17731669412051608590)
XLA Ops:
  0.6 75.5 %factors.1 = (f32[32,2304]{1,0:T(8,128)S(1)}, f32[1600]{0:T(1024)S(1)}, f32[1600]{0:T(1024)S(1)}, bf16[100,128]{1,0:T(8,128)(2,1)S(1)}, f32[256,2304]{1,0:T(8,12...) custom-call(f32[256,2048]{1,0:T(8,128)} %bitcast.11, ...), custom_call_target="tpu_custom_call" | custom-call | tf_op jit(solution)/shard_map/factors/pallas_call | solution.py:554
  76.2 6.0 %write.1 = (bf16[2048,2048]{1,0:T(8,128)(2,1)}, bf16[2048,256]{1,0:T(8,128)(2,1)}, f32[256,2048]{1,0:T(8,128)}, f32[256,256]{1,0:T(8,128)}, f32[256,2048]{1,0:T(...) custom-call(f32[32,2304]{1,0:T(8,128)S(1)} %get-tuple-element.34.ref, ...), custom_call_target="tpu_custom_call" | custom-call | tf_op jit(solution)/shard_map/write/pallas_call | solution.py:622

commit v4 on v3

--- a/solution.py
+++ b/solution.py
@@ -110,14 +110,23 @@
     right_all,
     basis_in,
     vector_in,
+    base_send,
+    base_recv,
+    ortho_all,
+    factor_all,
+    right_cat,
     first_sem,
     load_sem,
     rep_send,
     rep_recv,
     grp_send,
     grp_recv,
+    base_sems,
+    ortho_sems,
     x_send,
     x_recv,
+    far_core_send,
+    far_core_recv,
     plane_send,
     plane_recv,
     core_send,
@@ -245,9 +254,55 @@
 
     pl.semaphore_wait(barrier, reps - 1 + grps - 1)
 
+    side = 4
+    y, z, x, core = me // side, me % side, my // 2, my % 2
+    place = (y, z)
+    block = grad_query.shape[0]
+    near = block * 3 // 4
+    strip = near // side
+    rest = block - near
+    wide = (columns + gate) // 2
+    cut = -(-wide // 256) * 128
+
+    def wrap(value):
+        return lax.rem(value + 2 * side, side)
+
+    def send_base(k, part, source, hop):
+        return pltpu.make_async_remote_copy(
+            src_ref=source,
+            dst_ref=base_recv.at[k, part],
+            send_sem=base_sems.at[0, k, part],
+            recv_sem=base_sems.at[1, k, part],
+            device_id={"grp": wrap(x + hop) * 2 + core},
+        )
+
+    def send_ortho(k):
+        return pltpu.make_async_remote_copy(
+            src_ref=ortho_all.at[0],
+            dst_ref=ortho_all.at[k],
+            send_sem=ortho_sems.at[0, k],
+            recv_sem=ortho_sems.at[1, k],
+            device_id={"grp": wrap(x + k) * 2 + core},
+        )
+
+    sends = []
+
+    def begin(*copies):
+        for copy in copies:
+            copy.start()
+            sends.append(copy)
+
     start_1, recv_1, send_1 = to_peers(0, "rep", lambda peer: left_send.at[peer], left_recv)
     start_1()
     left_recv[me] = left_send[me]
+
+    for copy in later:
+        copy.wait()
+    for part in (0, 1):
+        at = slice(part * wide, (part + 1) * wide)
+        those = pl.ds(pl.multiple_of(place[part] * strip, 16), strip)
+        base_send[part] = master_in[those, at] - 0.45 * momentum_in[those, at]
+    begin(*[send_base(k, 0, base_send.at[0], k) for k in (1, 3)])
     recv_1()
     total = left_recv[0]
     for i in range(1, reps):
@@ -290,6 +345,9 @@
     vector_all[my] = vector_send[...]
 
     recv_3()
+    begin(*[send_base(k, 1, base_send.at[1], k) for k in (1, 3)])
+    send_base(1, 0, base_send.at[0], 1).wait_recv()
+    begin(send_base(2, 0, base_recv.at[1, 0], 1))
     gram = gram_all[0]
     for i in range(1, grps):
         gram += gram_all[i]
@@ -300,6 +358,7 @@
     gate_gram = jnp.concatenate([quarters[2], quarters[3]], axis=0)
     inverse = inverse_roots(query_gram, gate_gram)
     ortho = full_dot(inverse, left[...])
+    ortho_all[0] = ortho
     ortho_high, ortho_low = split(ortho)
 
     rows = RANK // reps
@@ -314,6 +373,9 @@
     start_4, recv_4, send_4 = to_peers(2, "rep", lambda peer: right_send.at[peer], right_recv)
     start_4()
     right_recv[me] = right_send[me]
+    begin(*[send_ortho(k) for k in (1, 3, 2)])
+    send_base(3, 1, base_send.at[1], 3).wait_recv()
+    begin(send_base(2, 1, base_recv.at[3, 1], 3))
     recv_4()
     total = right_recv[0]
     for i in range(1, reps):
@@ -348,59 +410,84 @@
         )
     weight_out[...] = vector_place[0 : weight_out.shape[0], :].astype(BF16)
 
+    for k in range(side):
+        if k:
+            send_ortho(k).wait_recv()
+        for i in (0, 1):
+            high, low = split(ortho_all[k, i * RANK : (i + 1) * RANK].T / reps)
+            factor_all[k, i] = jnp.concatenate([high, high, low], axis=1)
+    for k, part in ((3, 0), (1, 1), (2, 0), (2, 1)):
+        send_base(k, part, base_send.at[part], 1).wait_recv()
+
     recv_6()
     for i in range(reps):
         right_out[i * rows : (i + 1) * rows, :] = right_all[i]
-
-    for copy in later:
-        copy.wait()
-    block = grad_query.shape[0]
-    factors = []
-    for part in (slice(0, RANK), slice(RANK, BOTH)):
-        high, low = split(ortho[part].T / reps)
-        factors.append(jnp.concatenate([high, high, low], axis=1))
-    own_rows = pl.ds(pl.multiple_of(my * block, block), block)
-    tiles = [(start, 256) for start in range(0, columns + gate, 256)]
-    for start, size in tiles:
+    for start, size, _ in pieces:
         at = slice(start, start + size)
         high, low = split(right_out[:, at])
-        approx = mm(
-            factors[0 if start < columns else 1],
-            jnp.concatenate([high, low, high], axis=0),
-        )
-        new_error[:, at] = approx
-        moved = 0.9 * momentum_in[:, at] + approx
-        new_momentum[:, at] = moved
-        updated = master_in[:, at] - 0.5 * moved
-        new_master[:, at] = updated
-        weights[own_rows, at] = updated.astype(BF16)
-
-    side = 4
-    y, z, x, core = me // side, me % side, my // 2, my % 2
-    half = block // 2
-    strip = half // side
-
-    def move(row, size, send, recv, **peer):
-        span = weights.at[pl.ds(pl.multiple_of(row, strip // 2), size)]
+        right_cat[:, at] = jnp.concatenate([high, low, high], axis=0)
+
+    own_row = my * block
+
+    def finish(first_row, count):
+        those = slice(first_row, first_row + count)
+        into = pl.ds(pl.multiple_of(own_row + first_row, 16), count)
+        for start in range(0, columns + gate, 256):
+            at = slice(start, start + 256)
+            approx = mm(
+                factor_all[0, 0 if start < columns else 1, those, :], right_cat[:, at]
+            )
+            new_error[those, at] = approx
+            old = momentum_in[those, at]
+            new_momentum[those, at] = 0.9 * old + approx
+            updated = (master_in[those, at] - 0.45 * old) - 0.5 * approx
+            new_master[those, at] = updated
+            weights[into, at] = updated.astype(BF16)
+
+    def strip_weights(k, part):
+        those = pl.ds(pl.multiple_of(place[part] * strip, 16), strip)
+        into = pl.ds(pl.multiple_of(rows_of(wrap(x - k), core, place[part]), 16), strip)
+        low, high = part * wide, (part + 1) * wide
+        bounds = [(low, min(high, columns), 0), (max(low, columns), high, 1)]
+        for start, end, which in bounds:
+            if start < end:
+                approx = mm(factor_all[k, which, those, :], right_cat[:, start:end])
+                base = base_recv[k, part, :, start - low : end - low]
+                weights[into, start:end] = (base - 0.5 * approx).astype(BF16)
+
+    def move(row, size, start, width, send, recv, **peer):
+        span = weights.at[pl.ds(pl.multiple_of(row, 16), size), pl.ds(start, width)]
         return pltpu.make_async_remote_copy(
             src_ref=span, dst_ref=span, send_sem=send, recv_sem=recv, device_id=peer
         )
 
-    def rows_of(from_x, from_core, part, at):
-        return (from_x * 2 + from_core) * block + part * half + at * strip
-
-    def wrap(value):
-        return lax.rem(value + 2 * side, side)
-
-    place = (y, z)
-
-    def along_x(k, part, from_x, hop):
+    def rows_of(from_x, from_core, at):
+        return (from_x * 2 + from_core) * block + at * strip
+
+    def columns_of(part, j):
+        low = part * wide
+        return {2: (low, cut), 0: (low + cut, wide - cut)}.get(j, (low, wide))
+
+    far = ((1, 0, rest), (3, 0, rest), (2, 0, rest // 2), (2, rest // 2, rest // 2))
+
+    def far_span(slot, from_x, from_core):
+        _, offset, size = far[slot]
+        return rows_of(from_x, from_core, 0) + near + offset, size, 0, columns + gate
+
+    def along_x(slot, from_x, hop):
         return move(
-            rows_of(from_x, core, part, place[part]),
-            strip,
-            x_send.at[k, part],
-            x_recv.at[k, part],
+            *far_span(slot, from_x, core),
+            x_send.at[slot],
+            x_recv.at[slot],
             grp=wrap(x + hop) * 2 + core,
+        )
+
+    def far_to_core(slot, from_core):
+        return move(
+            *far_span(slot, wrap(x - far[slot][0]), from_core),
+            far_core_send.at[slot],
+            far_core_recv.at[slot],
+            grp=x * 2 + 1 - core,
         )
 
     def in_plane(k, part, j, hop):
@@ -408,62 +495,55 @@
         return strip_move(k, part, j, offset, hop)
 
     def strip_move(k, part, j, offset, hop):
-        row = rows_of(wrap(x - k), core, part, wrap(place[part] + offset))
-        size = strip if j in (1, 3) else strip // 2
-        if j == 0:
-            row += strip // 2
         peer = (
             wrap(y + hop) * side + z if part == 0 else y * side + wrap(z + hop)
         )
         return move(
-            row, size, plane_send.at[k, part, j], plane_recv.at[k, part, j], rep=peer
+            rows_of(wrap(x - k), core, wrap(place[part] + offset)),
+            strip,
+            *columns_of(part, j),
+            plane_send.at[k, part, j],
+            plane_recv.at[k, part, j],
+            rep=peer,
         )
 
     landed = {1: -1, 3: 1, 2: -2, 0: -2}
 
     def to_core(k, part, j, from_core):
-        row = rows_of(
-            wrap(x - k), from_core, part, wrap(place[part] + landed.get(j, 0))
-        )
-        if j == 0:
-            row += strip // 2
         return move(
-            row,
-            strip // 2 if j in (0, 2) else strip,
+            rows_of(wrap(x - k), from_core, wrap(place[part] + landed.get(j, 0))),
+            strip,
+            *columns_of(part, j),
             core_send.at[k, part, j],
             core_recv.at[k, part, j],
             grp=x * 2 + 1 - core,
         )
 
-    def own_to_core(part, from_core):
+    def own_to_core(from_core):
         return move(
-            rows_of(x, from_core, part, 0),
-            half,
-            core_send.at[0, part, 0],
-            core_recv.at[0, part, 0],
+            rows_of(x, from_core, 0),
+            block,
+            0,
+            columns + gate,
+            core_send.at[0, 0, 0],
+            core_recv.at[0, 0, 0],
             grp=x * 2 + 1 - core,
         )
 
-    sends = [along_x(1, 0, x, 1), along_x(3, 1, x, 3), along_x(1, 1, x, 1), along_x(3, 0, x, 3)]
-    sends += [own_to_core(0, core), own_to_core(1, core)]
-    for copy in sends:
-        copy.start()
-    for start, size in tiles:
-        at = slice(start, start + size)
-        new_error[:, at] = (grad_in[:, at] + error_in[:, at]) - new_error[:, at]
-
-    def begin(*copies):
-        for copy in copies:
-            copy.start()
-            sends.append(copy)
-
-    def from_x(k, part):
-        along_x(k, part, wrap(x - k), 0).wait_recv()
-        if (k, part) in ((1, 0), (3, 1)):
-            begin(along_x(2, part, wrap(x - k), k))
+    finish(near, rest)
+    begin(along_x(0, x, 1), along_x(1, x, 3))
+    order = [(k, part) for k in (1, 3, 2) for part in (0, 1)]
+    for k, part in order:
+        strip_weights(k, part)
         begin(
             in_plane(k, part, 1, 1), in_plane(k, part, 3, 3), to_core(k, part, 4, core)
         )
+    finish(0, near)
+    begin(own_to_core(core))
+
+    for slot, hop in ((0, 1), (1, 3)):
+        along_x(slot, wrap(x - far[slot][0]), hop).wait_recv()
+        begin(along_x(slot + 2, wrap(x - far[slot][0]), hop), far_to_core(slot, core))
 
     def from_neighbours(k, part):
         for j, relayed in ((1, 2), (3, 0)):
@@ -475,24 +555,26 @@
             strip_move(k, part, j, landed[j], 1).wait_recv()
             begin(to_core(k, part, j, core))
 
-    for k, part in ((1, 0), (3, 1), (3, 0), (1, 1)):
-        from_x(k, part)
-    for k, part in ((1, 0), (3, 1), (3, 0), (1, 1)):
+    def errors(start):
+        at = slice(start, start + 256)
+        new_error[:, at] = (grad_in[:, at] + error_in[:, at]) - new_error[:, at]
+
+    tiles = list(range(0, columns + gate, 256))
+    for i, (k, part) in enumerate(order):
         from_neighbours(k, part)
-    for part in (0, 1):
-        from_x(2, part)
-    for k, part in ((1, 0), (3, 1), (3, 0), (1, 1)):
+        for start in tiles[i :: len(order)]:
+            errors(start)
+    for k, part in order:
         from_opposite(k, part)
-    for part in (0, 1):
-        from_neighbours(2, part)
-    for part in (0, 1):
-        from_opposite(2, part)
-    for part in (0, 1):
-        own_to_core(part, 1 - core).wait_recv()
-    for k in (1, 3, 2):
-        for part in (0, 1):
-            for j in range(5):
-                to_core(k, part, j, 1 - core).wait_recv()
+    for slot in (2, 3):
+        along_x(slot, wrap(x - 2), 1).wait_recv()
+        begin(far_to_core(slot, core))
+    own_to_core(1 - core).wait_recv()
+    for slot in range(4):
+        far_to_core(slot, 1 - core).wait_recv()
+    for k, part in order:
+        for j in range(5):
+            to_core(k, part, j, 1 - core).wait_recv()
     for copy in sends:
         copy.wait_send()
     for wait in (send_1, send_2, send_3, send_v, send_4, send_5, send_6):
@@ -580,14 +662,23 @@
             VMEM((reps, share, both), F32),
             VMEM((RANK, both), F32),
             VMEM((1, length), F32),
+            VMEM((2, rows * 3 // 16, both // 2), F32),
+            VMEM((4, 2, rows * 3 // 16, both // 2), F32),
+            VMEM((4, BOTH, rows), F32),
+            VMEM((4, 2, rows, 3 * RANK), BF16),
+            VMEM((3 * RANK, both), BF16),
             pltpu.SemaphoreType.DMA((3,)),
             pltpu.SemaphoreType.DMA((4, columns // 512 + 1)),
             pltpu.SemaphoreType.DMA((4, reps)),
             pltpu.SemaphoreType.DMA((4, reps)),
             pltpu.SemaphoreType.DMA((3, grps)),
             pltpu.SemaphoreType.DMA((3, grps)),
-            pltpu.SemaphoreType.DMA((4, 2)),
-            pltpu.SemaphoreType.DMA((4, 2)),
+            pltpu.SemaphoreType.DMA((2, 4, 2)),
+            pltpu.SemaphoreType.DMA((2, 4)),
+            pltpu.SemaphoreType.DMA((4,)),
+            pltpu.SemaphoreType.DMA((4,)),
+            pltpu.SemaphoreType.DMA((4,)),
+            pltpu.SemaphoreType.DMA((4,)),
             pltpu.SemaphoreType.DMA((4, 2, 4)),
             pltpu.SemaphoreType.DMA((4, 2, 4)),
             pltpu.SemaphoreType.DMA((4, 2, 5)),

time: 82.4 us -> 74.6 us (0.905)
  Pallas kernels: 81.6 us -> 73.8 us
    pallas_call x1, Pallas kernels: 75.5 us -> 67.7 us  [per_device(): pl.pallas_call(functools.partial(factor_kernel, reps, grps), out_shape=tu...]
where the time goes in v4:
time: 74.6 us; the launch traced here: 74.4 us
  Pallas kernels  73.8 us (99%)
    pallas_call x1, Pallas kernels, per_device(): pl.pallas_call(functools.partial(factor_kernel, reps, grps), out_shape=tu...  67.7 us
    pallas_call x1, Pallas kernels, per_device(): pl.pallas_call(functools.partial(write_kernel, columns), out_shape=shapes...  6.04 us

profile of v4, /device:TPU:1, one launch (start us, length us, event | category | flops | bytes accessed | tf_op | source)
XLA Modules:
  0.0 74.4 jit_solution(15619095070122810009)
XLA Ops:
  0.6 67.7 %factors.1 = (f32[32,2304]{1,0:T(8,128)S(1)}, f32[1600]{0:T(1024)S(1)}, f32[1600]{0:T(1024)S(1)}, bf16[100,128]{1,0:T(8,128)(2,1)S(1)}, f32[256,2304]{1,0:T(8,12...) custom-call(f32[256,2048]{1,0:T(8,128)} %bitcast.11, ...), custom_call_target="tpu_custom_call" | custom-call | tf_op jit(solution)/shard_map/factors/pallas_call | solution.py:636
  68.4 6.0 %write.1 = (bf16[2048,2048]{1,0:T(8,128)(2,1)}, bf16[2048,256]{1,0:T(8,128)(2,1)}, f32[256,2048]{1,0:T(8,128)}, f32[256,256]{1,0:T(8,128)}, f32[256,2048]{1,0:T(...) custom-call(f32[32,2304]{1,0:T(8,128)S(1)} %get-tuple-element.34.ref, ...), custom_call_target="tpu_custom_call" | custom-call | tf_op jit(solution)/shard_map/write/pallas_call | solution.py:713

commit v5 on v4

--- a/solution.py
+++ b/solution.py
@@ -110,6 +110,7 @@
     right_all,
     basis_in,
     vector_in,
+    base_in,
     base_send,
     base_recv,
     ortho_all,
@@ -121,6 +122,7 @@
     rep_recv,
     grp_send,
     grp_recv,
+    strip_sems,
     base_sems,
     ortho_sems,
     x_send,
@@ -155,6 +157,65 @@
             ),
         )
 
+    side = 4
+    y, z, x, core = me // side, me % side, my // 2, my % 2
+    place = (y, z)
+    block = grad_query.shape[0]
+    near = block * 3 // 4
+    strip = near // side
+    rest = block - near
+    wide = (columns + gate) // 2
+    cut = -(-wide // 256) * 128
+
+    def wrap(value):
+        return lax.rem(value + 2 * side, side)
+
+    def send_base(k, part, source, hop):
+        return pltpu.make_async_remote_copy(
+            src_ref=source,
+            dst_ref=base_recv.at[k, part],
+            send_sem=base_sems.at[0, k, part],
+            recv_sem=base_sems.at[1, k, part],
+            device_id={"grp": wrap(x + hop) * 2 + core},
+        )
+
+    def send_ortho(k):
+        return pltpu.make_async_remote_copy(
+            src_ref=ortho_all.at[0],
+            dst_ref=ortho_all.at[k],
+            send_sem=ortho_sems.at[0, k],
+            recv_sem=ortho_sems.at[1, k],
+            device_id={"grp": wrap(x + k) * 2 + core},
+        )
+
+    sends = []
+
+    def begin(*copies):
+        for copy in copies:
+            copy.start()
+            sends.append(copy)
+
+    strips = []
+    for part in (0, 1):
+        those = pl.ds(pl.multiple_of(place[part] * strip, 16), strip)
+        low, high = part * wide, (part + 1) * wide
+        for i, pair in enumerate(
+            ((momentum_query, momentum_gate), (master_query, master_gate))
+        ):
+            for j, (start, end) in enumerate(
+                ((low, min(high, columns)), (max(low, columns), high))
+            ):
+                if start < end:
+                    strips.append(
+                        pltpu.make_async_copy(
+                            pair[j].at[those, pl.ds(start - j * columns, end - start)],
+                            base_in.at[part, i, :, pl.ds(start - low, end - start)],
+                            strip_sems.at[part, i, j],
+                        )
+                    )
+    for copy in strips:
+        copy.start()
+
     first = [
         pltpu.make_async_copy(basis_query, basis_in.at[:, pl.ds(0, columns)], first_sem.at[0]),
         pltpu.make_async_copy(basis_gate, basis_in.at[:, pl.ds(columns, gate)], first_sem.at[1]),
@@ -226,6 +287,14 @@
     left_query = jnp.zeros((RANK, grad_query.shape[0]), F32)
     left_gate = left_query
     for start, size, index in pieces:
+        if index == 1:
+            for copy in strips:
+                copy.wait()
+            for part in (0, 1):
+                base_send[part] = base_in[part, 1] - 0.45 * base_in[part, 0]
+            pl.semaphore_wait(barrier, reps - 1 + grps - 1)
+            for k, part in ((1, 0), (3, 1), (3, 0), (1, 1)):
+                begin(send_base(k, part, base_send.at[part], k))
         for copy in loads(start, size, index):
             copy.wait()
         at = slice(start, start + size)
@@ -252,62 +321,15 @@
         width = min(128, length - i * 128)
         left_send[i, share : share + 1, 0:width] = vector_in[:, i * 128 : i * 128 + width]
 
-    pl.semaphore_wait(barrier, reps - 1 + grps - 1)
-
-    side = 4
-    y, z, x, core = me // side, me % side, my // 2, my % 2
-    place = (y, z)
-    block = grad_query.shape[0]
-    near = block * 3 // 4
-    strip = near // side
-    rest = block - near
-    wide = (columns + gate) // 2
-    cut = -(-wide // 256) * 128
-
-    def wrap(value):
-        return lax.rem(value + 2 * side, side)
-
-    def send_base(k, part, source, hop):
-        return pltpu.make_async_remote_copy(
-            src_ref=source,
-            dst_ref=base_recv.at[k, part],
-            send_sem=base_sems.at[0, k, part],
-            recv_sem=base_sems.at[1, k, part],
-            device_id={"grp": wrap(x + hop) * 2 + core},
-        )
-
-    def send_ortho(k):
-        return pltpu.make_async_remote_copy(
-            src_ref=ortho_all.at[0],
-            dst_ref=ortho_all.at[k],
-            send_sem=ortho_sems.at[0, k],
-            recv_sem=ortho_sems.at[1, k],
-            device_id={"grp": wrap(x + k) * 2 + core},
-        )
-
-    sends = []
-
-    def begin(*copies):
-        for copy in copies:
-            copy.start()
-            sends.append(copy)
-
     start_1, recv_1, send_1 = to_peers(0, "rep", lambda peer: left_send.at[peer], left_recv)
     start_1()
     left_recv[me] = left_send[me]
-
-    for copy in later:
-        copy.wait()
-    for part in (0, 1):
-        at = slice(part * wide, (part + 1) * wide)
-        those = pl.ds(pl.multiple_of(place[part] * strip, 16), strip)
-        base_send[part] = master_in[those, at] - 0.45 * momentum_in[those, at]
-    begin(*[send_base(k, 0, base_send.at[0], k) for k in (1, 3)])
     recv_1()
     total = left_recv[0]
     for i in range(1, reps):
         total += left_recv[i]
     left_sum[...] = total
+
 
     start_2, recv_2, send_2 = to_peers(1, "rep", lambda peer: left_sum, left_all)
     start_2()
@@ -345,9 +367,9 @@
     vector_all[my] = vector_send[...]
 
     recv_3()
-    begin(*[send_base(k, 1, base_send.at[1], k) for k in (1, 3)])
-    send_base(1, 0, base_send.at[0], 1).wait_recv()
-    begin(send_base(2, 0, base_recv.at[1, 0], 1))
+    for k, part in ((1, 0), (3, 1)):
+        send_base(k, part, base_send.at[part], k).wait_recv()
+        begin(send_base(2, part, base_recv.at[k, part], k))
     gram = gram_all[0]
     for i in range(1, grps):
         gram += gram_all[i]
@@ -374,8 +396,6 @@
     start_4()
     right_recv[me] = right_send[me]
     begin(*[send_ortho(k) for k in (1, 3, 2)])
-    send_base(3, 1, base_send.at[1], 3).wait_recv()
-    begin(send_base(2, 1, base_recv.at[3, 1], 3))
     recv_4()
     total = right_recv[0]
     for i in range(1, reps):
@@ -419,6 +439,8 @@
     for k, part in ((3, 0), (1, 1), (2, 0), (2, 1)):
         send_base(k, part, base_send.at[part], 1).wait_recv()
 
+    for copy in later:
+        copy.wait()
     recv_6()
     for i in range(reps):
         right_out[i * rows : (i + 1) * rows, :] = right_all[i]
@@ -662,6 +684,7 @@
             VMEM((reps, share, both), F32),
             VMEM((RANK, both), F32),
             VMEM((1, length), F32),
+            VMEM((2, 2, rows * 3 // 16, both // 2), F32),
             VMEM((2, rows * 3 // 16, both // 2), F32),
             VMEM((4, 2, rows * 3 // 16, both // 2), F32),
             VMEM((4, BOTH, rows), F32),
@@ -673,6 +696,7 @@
             pltpu.SemaphoreType.DMA((4, reps)),
             pltpu.SemaphoreType.DMA((3, grps)),
             pltpu.SemaphoreType.DMA((3, grps)),
+            pltpu.SemaphoreType.DMA((2, 2, 2)),
             pltpu.SemaphoreType.DMA((2, 4, 2)),
             pltpu.SemaphoreType.DMA((2, 4)),
             pltpu.SemaphoreType.DMA((4,)),

time: 74.6 us -> 72.1 us (0.966)
  Pallas kernels: 73.8 us -> 71.2 us
    pallas_call x1, Pallas kernels: 67.7 us -> 65.2 us  [per_device(): pl.pallas_call(functools.partial(factor_kernel, reps, grps), out_shape=tu...]
where the time goes in v5:
time: 72.1 us; the launch traced here: 71.9 us
  Pallas kernels  71.2 us (99%)
    pallas_call x1, Pallas kernels, per_device(): pl.pallas_call(functools.partial(factor_kernel, reps, grps), out_shape=tu...  65.2 us
    pallas_call x1, Pallas kernels, per_device(): pl.pallas_call(functools.partial(write_kernel, columns), out_shape=shapes...  6.04 us

profile of v5, /device:TPU:1, one launch (start us, length us, event | category | flops | bytes accessed | tf_op | source)
XLA Modules:
  0.0 71.9 jit_solution(18324519025407019779)
XLA Ops:
  0.6 65.2 %factors.1 = (f32[32,2304]{1,0:T(8,128)S(1)}, f32[1600]{0:T(1024)S(1)}, f32[1600]{0:T(1024)S(1)}, bf16[100,128]{1,0:T(8,128)(2,1)S(1)}, f32[256,2304]{1,0:T(8,12...) custom-call(f32[256,2048]{1,0:T(8,128)} %bitcast.11, ...), custom_call_target="tpu_custom_call" | custom-call | tf_op jit(solution)/shard_map/factors/pallas_call | solution.py:658
  65.8 6.0 %write.1 = (bf16[2048,2048]{1,0:T(8,128)(2,1)}, bf16[2048,256]{1,0:T(8,128)(2,1)}, f32[256,2048]{1,0:T(8,128)}, f32[256,256]{1,0:T(8,128)}, f32[256,2048]{1,0:T(...) custom-call(f32[32,2304]{1,0:T(8,128)S(1)} %get-tuple-element.34.ref, ...), custom_call_target="tpu_custom_call" | custom-call | tf_op jit(solution)/shard_map/write/pallas_call | solution.py:737

commit v6 on v5

--- a/solution.py
+++ b/solution.py
@@ -552,10 +552,11 @@
             grp=x * 2 + 1 - core,
         )
 
-    finish(near, rest)
-    begin(along_x(0, x, 1), along_x(1, x, 3))
     order = [(k, part) for k in (1, 3, 2) for part in (0, 1)]
     for k, part in order:
+        if (k, part) == (3, 0):
+            finish(near, rest)
+            begin(along_x(0, x, 1), along_x(1, x, 3))
         strip_weights(k, part)
         begin(
             in_plane(k, part, 1, 1), in_plane(k, part, 3, 3), to_core(k, part, 4, core)

time: 72.1 us -> 72.4 us (level)
  no operation moved by 1% of the time
where the time goes in v6:
time: 72.4 us; the launch traced here: 72.2 us
  Pallas kernels  71.6 us (99%)
    pallas_call x1, Pallas kernels, per_device(): pl.pallas_call(functools.partial(factor_kernel, reps, grps), out_shape=tu...  65.5 us
    pallas_call x1, Pallas kernels, per_device(): pl.pallas_call(functools.partial(write_kernel, columns), out_shape=shapes...  6.04 us

profile of v6, /device:TPU:1, one launch (start us, length us, event | category | flops | bytes accessed | tf_op | source)
XLA Modules:
  0.0 72.2 jit_solution(2984746018319750717)
XLA Ops:
  0.6 65.5 %factors.1 = (f32[32,2304]{1,0:T(8,128)S(1)}, f32[1600]{0:T(1024)S(1)}, f32[1600]{0:T(1024)S(1)}, bf16[100,128]{1,0:T(8,128)(2,1)S(1)}, f32[256,2304]{1,0:T(8,12...) custom-call(f32[256,2048]{1,0:T(8,128)} %bitcast.11, ...), custom_call_target="tpu_custom_call" | custom-call | tf_op jit(solution)/shard_map/factors/pallas_call | solution.py:659
  66.2 6.0 %write.1 = (bf16[2048,2048]{1,0:T(8,128)(2,1)}, bf16[2048,256]{1,0:T(8,128)(2,1)}, f32[256,2048]{1,0:T(8,128)}, f32[256,256]{1,0:T(8,128)}, f32[256,2048]{1,0:T(...) custom-call(f32[32,2304]{1,0:T(8,128)S(1)} %get-tuple-element.34.ref, ...), custom_call_target="tpu_custom_call" | custom-call | tf_op jit(solution)/shard_map/write/pallas_call | solution.py:738
